TPU v7x, 128 devices: a whole 4x4x4 slice. The times are simulated.
128 devices in a mesh: section: 2 (over y_lo), dp: 4 (over x), shard: 16 (over y_hi, z, core).
Axes of the slice: x: 4, y: 4 (y_hi: 2, y_lo: 2; y = y_hi * 2 + y_lo), z: 4, core: 2. Of those that a mesh axis runs over, the one named last changes fastest.
Arguments:
- features: bfloat16 [2, 2048, 6144], P('section', ('dp', 'shard')), may hold values from -6 to 6
- delayed_error: bfloat16 [2, 2048, 6144], P('section', ('dp', 'shard')), may hold values from -6 to 6
- ln_gain: float32 [2, 6144], P('section'), may hold values from 0.25 to 1.75
- w_in: bfloat16 [2, 6144, 12288], P('section', None, 'shard'), may hold values from -0.078125 to 0.078125
- w_out: bfloat16 [2, 12288, 6144], P('section', 'shard'), may hold values from -0.0546875 to 0.0546875
Outputs:
- passed_error: bfloat16 [2, 2048, 6144], P('section', ('dp', 'shard'))
- gain_grad: float32 [2, 6144], P('section')
- w_in_grad: bfloat16 [2, 6144, 12288], P('section', 'dp', 'shard')
- w_out_grad: bfloat16 [2, 12288, 6144], P('section', 'shard', 'dp')
All inputs are finite; a program needn't handle non-finite values.
Results may differ from a plain program's by a relative error of at most 0.013.
Values may be sent and summed in bfloat16 or wider, within the bound.
A program may use at most 192 MiB of HBM per device.

v0:
```python
import jax
import jax.numpy as jnp
from jax import lax
from jax.sharding import PartitionSpec as P

SQRT_HALF = 0.7071067811865476
INV_ROOT_TWO_PI = 0.3989422804014327
EPSILON = 1e-06


def shifted(block, axis, distance):
    devices = range(lax.axis_size(axis))
    route = [((i - distance) % len(devices), i) for i in devices]
    return lax.ppermute(block, axis, route)


def per_device(features, delayed_error, ln_gain, w_in, w_out):
    tokens_here = features[0]
    errors = delayed_error[0]
    scale = ln_gain[0]
    in_block = w_in[0]
    out_block = w_out[0]
    values = tokens_here.astype(jnp.float32)
    average = jnp.mean(values, -1, keepdims=True)
    centred = values - average
    variance = jnp.mean(centred * centred, -1, keepdims=True)
    inverse = lax.rsqrt(variance + EPSILON)
    centred = centred * inverse
    normed = (centred * scale).astype(jnp.bfloat16)
    normed_group, error_group = (
        lax.all_gather(normed, "shard", axis=0, tiled=True),
        lax.all_gather(errors, "shard", axis=0, tiled=True),
    )
    pre = jnp.dot(normed_group, in_block, preferred_element_type=jnp.float32)
    normal_cdf = 0.5 * (1.0 + jax.scipy.special.erf(pre * SQRT_HALF))
    density = INV_ROOT_TWO_PI * jnp.exp(-0.5 * pre * pre)
    active = (pre * normal_cdf).astype(jnp.bfloat16)
    back_act = jnp.einsum("td,fd->tf", error_group, out_block, preferred_element_type=jnp.float32)
    pre_error = (back_act * (normal_cdf + pre * density)).astype(jnp.bfloat16)
    norm_error = lax.psum_scatter(
        jnp.einsum("tf,df->td", pre_error, in_block, preferred_element_type=jnp.float32).astype(
            jnp.bfloat16
        ),
        "shard",
        scatter_dimension=0,
        tiled=True,
    ).astype(jnp.float32)
    scaled = norm_error * scale
    corrected = inverse * (
        scaled
        - jnp.mean(scaled, -1, keepdims=True)
        - centred * jnp.mean(scaled * centred, -1, keepdims=True)
    )
    own_error = (errors.astype(jnp.float32) + corrected).astype(jnp.bfloat16)
    gain_grad = lax.psum(jnp.sum(norm_error * centred, 0), ("dp", "shard"))
    passed = shifted(own_error, "section", -1)
    in_part = jnp.dot(normed_group.T, pre_error, preferred_element_type=jnp.float32)
    out_part = jnp.einsum("tf,td->fd", active, error_group, preferred_element_type=jnp.float32)
    in_total, out_total = (
        lax.psum_scatter(
            in_part.astype(jnp.bfloat16), "dp", scatter_dimension=0, tiled=True
        ).astype(jnp.float32),
        lax.psum_scatter(
            out_part.astype(jnp.bfloat16), "dp", scatter_dimension=1, tiled=True
        ).astype(jnp.float32),
    )
    return (
        passed[None],
        gain_grad[None],
        in_total.astype(jnp.bfloat16)[None],
        out_total.astype(jnp.bfloat16)[None],
    )


def solution(mesh):
    return jax.shard_map(
        per_device,
        mesh=mesh,
        in_specs=(
            P("section", ("dp", "shard"), None),
            P("section", ("dp", "shard"), None),
            P("section", None),
            P("section", None, "shard"),
            P("section", "shard", None),
        ),
        out_specs=(
            P("section", ("dp", "shard"), None),
            P("section", None),
            P("section", "dp", "shard"),
            P("section", "shard", "dp"),
        ),
        check_vma=False,
    )
```

profile of v0, /device:TPU:0, one launch (start us, length us, event | category | flops | bytes accessed | tf_op | source)
XLA Modules:
  0.0 594.6 jit_solution(8329351901476849231)
XLA Ops:
  7.2 0.0 all-gather.4.cloned.1.call-start
  7.2 1.2 convert_reduce_fusion
  8.4 1.3 fusion.34
  9.7 1.9 fusion.29
  11.6 0.0 all-gather.4.cloned.1.call-update
  11.6 0.0 all-gather.6.cloned.1.call-start
  11.7 0.7 all-gather.6.cloned.1.call-update
  12.4 0.0 reduce-scatter.4.cloned.1.call-start
  12.4 65.7 %all-gather.4.cloned.1.call-done = bf16[512,6144]{1,0:T(8,128)(2,1)} async-done(((bf16[32,6144]{1,0:T(8,128)(2,1)}), bf16[512,6144]{1,0:T(8,128)(2,1)}) %all-gather.4.cloned.1.call-update) | async-done | bytes 6291472 | tf_op jit(solution)/shard_map/all_gather | solution.py:31
  78.1 9.4 %fusion.2 = f32[512,768]{1,0:T(8,128)S(1)} fusion(bf16[512,6144]{1,0:T(8,128)(2,1)} %all-gather.4.cloned.1.call-done, bf16[1,6144,768]{2,1,0:T(8,128)(2,1)} %param.8), kind=kOutput, calls=%fused_computation.4 | convolution fusion | flops 4831838208 | bytes 17301504 | tf_op jit(solution)/shard_map/dot_general | solution.py:34
  87.5 54.7 %all-gather.6.cloned.1.call-done = bf16[1,512,6144]{2,1,0:T(8,128)(2,1)} async-done(((bf16[1,32,6144]{2,1,0:T(8,128)(2,1)}), bf16[1,512,6144]{2,1,0:T(8,128)(2,1)}) %all-gather.6.cloned.1.call-update) | async-done | bytes 6291472 | tf_op jit(solution)/shard_map/all_gather | solution.py:32
  142.1 10.2 %fusion.16 = bf16[512,768]{1,0:T(8,128)(2,1)S(1)} fusion(f32[512,768]{1,0:T(8,128)S(1)} %fusion.2, bf16[1,768,6144]{2,1,0:T(8,128)(2,1)} %param.9, bf16[1,512,6144]{2,1,0:T(8,128)(2,1)} %all-gather.6.cloned.1.call-done), kind=kOutput, calls=%fused_computation.17 | convolution fusion | flops 4835770368 | bytes 18087936 | tf_op jit(solution)/shard_map/td,fd->tf/dot_general | solution.py:38
  152.3 10.8 %fusion.6 = bf16[512,6144]{1,0:T(8,128)(2,1)} fusion(bf16[512,768]{1,0:T(8,128)(2,1)S(1)} %fusion.16, bf16[1,6144,768]{2,1,0:T(8,128)(2,1)} %param.8), kind=kOutput, calls=%fused_computation.8 | convolution fusion | flops 4834983936 | bytes 16515072 | tf_op jit(solution)/shard_map/tf,df->td/dot_general | solution.py:41
  163.1 0.0 reduce-scatter.4.cloned.1.call-update
  163.1 0.0 reduce-scatter.8.cloned.1.call-start
  163.2 10.4 %convolution_convert_fusion.1 = bf16[768,6144]{1,0:T(8,128)(2,1)} fusion(bf16[1,512,6144]{2,1,0:T(8,128)(2,1)} %all-gather.6.cloned.1.call-done, f32[512,768]{1,0:T(8,128)S(1)} %fusion.2), kind=kOutput, calls=%fused_computation.1 | convolution fusion | flops 4838522880 | bytes 17301504 | tf_op jit(solution)/shard_map/tf,td->fd/dot_general | solution.py:58
  173.6 0.2 reduce-scatter.6.cloned.1.call-start
  173.8 10.7 %convolution_convert_fusion = bf16[6144,768]{1,0:T(8,128)(2,1)} fusion(bf16[512,6144]{1,0:T(8,128)(2,1)} %all-gather.4.cloned.1.call-done, bf16[512,768]{1,0:T(8,128)(2,1)S(1)} %fusion.16), kind=kOutput, calls=%fused_computation | convolution fusion | flops 4836556800 | bytes 16515072 | tf_op jit(solution)/shard_map/dot_general | solution.py:57
  184.6 66.3 %reduce-scatter.4.cloned.1.call-done = bf16[32,6144]{1,0:T(8,128)(2,1)} async-done(((bf16[512,6144]{1,0:T(8,128)(2,1)}), bf16[32,6144]{1,0:T(8,128)(2,1)}) %reduce-scatter.4.cloned.1.call-update) | async-done | bytes 393232 | tf_op jit(solution)/shard_map/reduce_scatter | solution.py:40
  250.9 1.5 fusion.36
  252.4 1.4 fusion.33
  253.7 0.7 collective-permute-start
  254.4 332.9 %psum.7 = f32[1,6144]{1,0:T(1,128)} all-reduce(f32[1,6144]{1,0:T(1,128)S(1)} %bitcast.67), channel_id=1, replica_groups=mesh['section'=2,'dp'=4,'shard'=16] {'dp','shard'}, use_global_device_ids=true, to_apply=%region_6.0 | all-reduce | flops 6144 | bytes 49152 | tf_op jit(solution)/shard_map/psum | solution.py:55
  587.3 0.7 copy.10
  (14 shorter events, 0.1 us)
Async XLA Ops:
  7.2 70.9 %all-gather.4.cloned.1.call-start = ((), (), s32[]{:S(2)}) async-start(), calls=%async_computation.3 | async-start | bytes 6684672 | tf_op jit(solution)/shard_map/all_gather | solution.py:31
  11.6 130.5 %all-gather.6.cloned.1.call-start = ((), (), s32[]{:S(2)}) async-start(), calls=%async_computation.7 | async-start | bytes 6684672 | tf_op jit(solution)/shard_map/all_gather | solution.py:32
  12.4 238.5 %reduce-scatter.4.cloned.1.call-start = ((), (), s32[]{:S(2)}) async-start(), calls=%async_computation.4 | async-start | bytes 6684672 | tf_op jit(solution)/shard_map/reduce_scatter | solution.py:40
  163.1 424.2 %reduce-scatter.8.cloned.1.call-start = ((), (), s32[]{:S(2)}) async-start(), calls=%async_computation.6 | async-start | bytes 11796480 | tf_op jit(solution)/shard_map/reduce_scatter | solution.py:63
  173.6 413.7 %reduce-scatter.6.cloned.1.call-start = ((), (), s32[]{:S(2)}) async-start(), calls=%async_computation.5 | async-start | bytes 11796480 | tf_op jit(solution)/shard_map/reduce_scatter | solution.py:60
  184.5 66.4 %copy-start = (bf16[1,32,6144]{2,1,0:T(8,128)(2,1)S(1)}, bf16[1,32,6144]{2,1,0:T(8,128)(2,1)}, u32[]{:S(2)}) copy-start(bf16[1,32,6144]{2,1,0:T(8,128)(2,1)} %param.5) | copy-start | bytes 1179652
  184.5 66.4 %copy-start.2 = (f32[1,6144]{1,0:T(1,128)S(1)}, f32[1,6144]{1,0:T(1,128)}, u32[]{:S(2)}) copy-start(f32[1,6144]{1,0:T(1,128)} %param.7) | copy-start | bytes 73732
  184.5 67.8 %copy-start.1 = (bf16[1,32,6144]{2,1,0:T(8,128)(2,1)S(1)}, bf16[1,32,6144]{2,1,0:T(8,128)(2,1)}, u32[]{:S(2)}) copy-start(bf16[1,32,6144]{2,1,0:T(8,128)(2,1)} %param.6) | copy-start | bytes 1179652
  253.7 333.6 %collective-permute-start = (bf16[32,6144]{1,0:T(8,128)(2,1)S(1)}, bf16[32,6144]{1,0:T(8,128)(2,1)S(1)}, u32[]{:S(2)}, u32[]{:S(2)}) collective-permute-start(bf16[32,6144]{1,0:T(8,128)(2,1)S(1)} %fusion.33), channel_id=1, source_target_pairs={{64,0},{0,64},{65,1},{1,65},{66,2},{2,66},{67,3},{3,67},{68,4},{4,... | collective-permute-start | bytes 1179656 | tf_op jit(solution)/shard_map/ppermute | solution.py:14
Sparse Core Ops, SparseCore 0:
  11.7 66.3 all-gather.3
  80.6 61.4 all-gather.5
  163.2 87.5 reduce-scatter.3
  253.8 87.7 reduce-scatter.7
  344.4 88.7 reduce-scatter.5
where the time goes:
time: 595 us
  blocking collectives  333 us (56%)
  waiting for transfers between devices  187 us (31%)
  matrix products  51.4 us (9%)
  between operations  13.8 us (2%)
  other arithmetic  7.2 us (1%)
    psum x1, blocking collectives, per_device(): gain_grad = lax.psum(jnp.sum(norm_error * centred, 0), ('dp', 'shard'))  333 us
    reduce_scatter x1, waiting for transfers between devices, per_device(): lax.psum_scatter(jnp.einsum('tf,df->td', pre_error, in_block, preferred_e...  66.3 us
    all_gather x1, waiting for transfers between devices, per_device(): lax.all_gather(normed, 'shard', axis=0, tiled=True)  65.7 us
    all_gather x1, waiting for transfers between devices, per_device(): lax.all_gather(errors, 'shard', axis=0, tiled=True)  54.7 us
  transfers between devices with their start and end apart: 6, of which 3 were waited for; matrix products, arithmetic and copies ran while one was open for 6% of the time, Pallas kernels for 0%

commit v1 on v0

v1 whole, which is shorter than its diff:
```python
import functools

import jax
import jax.numpy as jnp
from jax import lax
from jax.experimental import pallas as pl
from jax.experimental.pallas import tpu as pltpu
from jax.sharding import PartitionSpec as P

SQRT_HALF = 0.7071067811865476
INV_ROOT_TWO_PI = 0.3989422804014327
EPSILON = 1e-06
F32 = jnp.float32
BF16 = jnp.bfloat16
MESH = pl.DeviceIdType.MESH
W = 768
TOK = 32
GROUP = 512
PIECES = 8
LIMIT = 66_900_000

Y0, ZP, ZM, YZP, YZM, FA, FB, YFA, YFB = range(9)


def place():
    s = lax.axis_index("section")
    d = lax.axis_index("dp")
    j = lax.axis_index("shard")
    return s, d, j // 8, (j // 2) % 4, j % 2


def neighbour(dx=0, dh=0, dz=0, dc=0):
    s, d, h, z, c = place()
    return (
        s,
        (d + dx + 4) % 4,
        ((h + dh) % 2) * 8 + ((z + dz + 4) % 4) * 2 + (c + dc) % 2,
    )


def greet(barrier, targets):
    for target in targets:
        pl.semaphore_signal(barrier, inc=1, device_id=target, device_id_type=MESH)
    pl.semaphore_wait(barrier, len(targets))


def dot(a, b, ca, cb):
    return lax.dot_general(
        a, b, (((ca,), (cb,)), ((), ())), preferred_element_type=F32
    )


class Gather:
    def __init__(self, bufs, send, recv, core_recv):
        self.bufs, self.send, self.recv, self.core_recv = bufs, send, recv, core_recv

    def rows(self, dh, dz, dc=0, first=0, count=TOK):
        _, _, h, z, c = place()
        block = ((h + dh) % 2) * 8 + ((z + dz + 4) % 4) * 2 + (c + dc) % 2
        return pl.ds(pl.multiple_of(block * TOK + first, 16), count)

    def copy(self, p, a, rows, sem, target, source=None):
        there = self.bufs[a].at[p, rows, :]
        return pltpu.make_async_remote_copy(
            src_ref=there if source is None else source,
            dst_ref=there,
            send_sem=self.send.at[p, a],
            recv_sem=sem,
            device_id=target,
            device_id_type=MESH,
        )

    def put(self, p, a, rows, kind, target, source=None):
        self.copy(p, a, rows, self.recv.at[p, a, kind], target, source).start()

    def got(self, p, a, rows, kind):
        self.copy(p, a, rows, self.recv.at[p, a, kind], neighbour(dz=1)).wait_recv()

    def to_core(self, p, a, dh, dz, source=None):
        rows = self.rows(dh, dz)
        sem = self.core_recv.at[p, a, dh * 4 + dz % 4]
        self.copy(p, a, rows, sem, neighbour(dc=1), source).start()

    def stage0(self, p, sources):
        up, down, across = neighbour(dz=1), neighbour(dz=-1), neighbour(dh=1)
        own = self.rows(0, 0)
        for a in range(2):
            self.put(p, a, own, Y0, across, sources[a])
            self.put(p, a, own, ZM, up, sources[a])
            self.put(p, a, own, ZP, down, sources[a])
            self.to_core(p, a, 0, 0, sources[a])

    def stage1(self, p):
        up, down, across = neighbour(dz=1), neighbour(dz=-1), neighbour(dh=1)
        self.got(p, 0, self.rows(1, 0), Y0)
        self.put(p, 0, self.rows(1, 0), YZM, up)
        self.put(p, 0, self.rows(1, 0), YZP, down)
        self.to_core(p, 0, 1, 0)
        for a in range(2):
            self.got(p, a, self.rows(0, 1), ZP)
            self.put(p, a, self.rows(0, 1, 0, 0, 16), FA, down)
            self.to_core(p, a, 0, 1)
            self.got(p, a, self.rows(0, -1), ZM)
            self.put(p, a, self.rows(0, -1, 0, 16, 16), FB, up)
            self.to_core(p, a, 0, -1)
        self.put(p, 1, self.rows(0, 1), YZP, across)
        self.put(p, 1, self.rows(0, -1), YZM, across)
        self.got(p, 1, self.rows(1, 0), Y0)
        self.to_core(p, 1, 1, 0)

    def stage2(self, p):
        up, down, across = neighbour(dz=1), neighbour(dz=-1), neighbour(dh=1)
        self.got(p, 0, self.rows(1, 1), YZP)
        self.put(p, 0, self.rows(1, 1, 0, 0, 16), YFA, down)
        self.to_core(p, 0, 1, 1)
        self.got(p, 0, self.rows(1, -1), YZM)
        self.put(p, 0, self.rows(1, -1, 0, 16, 16), YFB, up)
        self.to_core(p, 0, 1, -1)
        for a in (1, 0):
            self.got(p, a, self.rows(0, 2, 0, 0, 16), FA)
            self.got(p, a, self.rows(0, 2, 0, 16, 16), FB)
            if a == 1:
                self.put(p, 1, self.rows(0, 2), YFA, across)
            self.to_core(p, a, 0, 2)
        self.got(p, 1, self.rows(1, 1), YZP)
        self.to_core(p, 1, 1, 1)
        self.got(p, 1, self.rows(1, -1), YZM)
        self.to_core(p, 1, 1, -1)

    def stage3(self, p):
        self.got(p, 0, self.rows(1, 2, 0, 0, 16), YFA)
        self.got(p, 0, self.rows(1, 2, 0, 16, 16), YFB)
        self.to_core(p, 0, 1, 2)
        self.got(p, 1, self.rows(1, 2), YFA)
        self.to_core(p, 1, 1, 2)

    def stage4(self, p):
        for a in range(2):
            for dh in range(2):
                for dz in range(4):
                    rows = self.rows(dh, dz, 1)
                    sem = self.core_recv.at[p, a, dh * 4 + dz]
                    self.copy(p, a, rows, sem, neighbour(dc=1)).wait_recv()

    def finish(self, p):
        for a in range(2):
            part = self.bufs[a].at[p, pl.ds(0, 480), :]
            pltpu.make_async_copy(part, part, self.send.at[p, a]).wait()


def gather_scratch(pieces):
    return [
        pltpu.SemaphoreType.DMA((pieces, 2)),
        pltpu.SemaphoreType.DMA((pieces, 2, 9)),
        pltpu.SemaphoreType.DMA((pieces, 2, 8)),
    ]


def forward_kernel(
    normed, errors, w_in, w_out,
    pre_error, active, own_normed, own_errors, slice_normed, slice_errors,
    all_normed, all_errors, win, wout, pre, back,
    send, recv, core_recv, x_send, x_recv, w_sem, own_sem,
):
    _, d, _, _, _ = place()
    weights = []
    for p in range(PIECES):
        cols = pl.ds(p * W, W)
        weights.append(
            (
                pltpu.make_async_copy(w_in.at[cols, :], win.at[p], w_sem.at[p, 0]),
                pltpu.make_async_copy(w_out.at[:, cols], wout.at[p], w_sem.at[p, 1]),
            )
        )
        for copy in weights[-1]:
            copy.start()
    gather = Gather((all_normed, all_errors), send, recv, core_recv)
    greet(
        pltpu.get_barrier_semaphore(),
        [neighbour(dx=1), neighbour(dx=-1), neighbour(dx=2), neighbour(dh=1)]
        + [neighbour(dz=1), neighbour(dz=-1), neighbour(dc=1)],
    )
    crossings = []
    for g, dx in enumerate((-1, 1, 2)):
        for half in range(2):
            cols = pl.ds(pl.multiple_of((((d + dx + 4) % 4) * 2 + half) * W, W), W)
            for a, (source, out) in enumerate(
                ((normed, slice_normed), (errors, slice_errors))
            ):
                copy = pltpu.make_async_remote_copy(
                    src_ref=source.at[:, cols],
                    dst_ref=out.at[g * 2 + half],
                    send_sem=x_send.at[g, half, a],
                    recv_sem=x_recv.at[g, half, a],
                    device_id=neighbour(dx=dx),
                    device_id_type=MESH,
                )
                copy.start()
                crossings.append(copy)
    pre[...] = jnp.zeros_like(pre)
    back[...] = jnp.zeros_like(back)

    @pl.loop(0, PIECES + 4)
    def _(t):
        @pl.when(t < PIECES)
        def _():
            cols = pl.ds(pl.multiple_of(t * W, W), W)
            gather.stage0(t, (normed.at[:, cols], errors.at[:, cols]))
            own = gather.rows(0, 0)
            all_normed[t, own, :] = normed[:, cols]
            all_errors[t, own, :] = errors[:, cols]

        @pl.when((t >= 1) & (t < PIECES + 1))
        def _():
            gather.stage1(t - 1)

        @pl.when((t >= 2) & (t < PIECES + 2))
        def _():
            gather.stage2(t - 2)

        @pl.when((t >= 3) & (t < PIECES + 3))
        def _():
            gather.stage3(t - 3)

        @pl.when(t >= 4)
        def _():
            p = t - 4
            gather.stage4(p)
            cols = pl.ds(pl.multiple_of(p * W, W), W)
            pltpu.make_async_copy(w_in.at[cols, :], win.at[p], w_sem.at[p, 0]).wait()
            pltpu.make_async_copy(w_out.at[:, cols], wout.at[p], w_sem.at[p, 1]).wait()
            pre[...] += dot(all_normed[p], win[p], 1, 0)
            back[...] += dot(all_errors[p], wout[p], 1, 1)

    own_copies = []
    for half in range(2):
        for a, (source, out) in enumerate(
            ((all_normed, own_normed), (all_errors, own_errors))
        ):
            copy = pltpu.make_async_copy(
                source.at[d * 2 + half], out.at[half], own_sem.at[half, a]
            )
            copy.start()
            own_copies.append(copy)

    @pl.loop(0, GROUP // 32)
    def _(i):
        rows = pl.ds(pl.multiple_of(i * 32, 32), 32)
        x = pre[rows, :]
        cdf = 0.5 * (1.0 + lax.erf(x * SQRT_HALF))
        density = INV_ROOT_TWO_PI * jnp.exp(-0.5 * x * x)
        active[rows, :] = (x * cdf).astype(BF16)
        pre_error[rows, :] = (back[rows, :] * (cdf + x * density)).astype(BF16)

    for copy in own_copies:
        copy.wait()
    for copy in crossings:
        copy.wait()

    @pl.loop(0, PIECES)
    def _(p):
        gather.finish(p)


def backward_kernel(
    pre_error, active, own_normed, own_errors, slice_normed, slice_errors, w_in,
    norm_error, in_grad, out_grad,
    all_normed, all_errors, acts, win, part, paired, summed, hop1, hop2, total, last,
    in_acc, out_acc,
    send, recv, core_recv, x_send, x_recv, f_send, f_recv, w_sem, own_sem,
    rs_send, rs_recv,
):
    _, _, h, z, c = place()
    gather = Gather((all_normed, all_errors), send, recv, core_recv)
    loads = []
    for half in range(2):
        for a, (source, buf) in enumerate(
            ((own_normed, all_normed), (own_errors, all_errors))
        ):
            loads.append(
                pltpu.make_async_copy(
                    source.at[half], buf.at[6 + half], own_sem.at[half, a]
                )
            )
    for copy in loads:
        copy.start()

    def weight(q):
        cols = pl.ds(pl.multiple_of(q * W, W), W)
        return pltpu.make_async_copy(w_in.at[cols, :], win.at[q], w_sem.at[q])

    for q in range(PIECES):
        weight(q).start()
    mine = (pre_error, active)
    up, down, left, right = (
        neighbour(dz=1), neighbour(dz=-1), neighbour(dx=-1), neighbour(dx=1),
    )
    across, other = neighbour(dh=1), neighbour(dc=1)
    greet(
        pltpu.get_barrier_semaphore(), [up, down, left, right, across, other]
    )
    low, high = pl.ds(0, 256), pl.ds(256, 256)

    def sideways(a, g, half):
        rows = pl.ds(half * 256, 256)
        return pltpu.make_async_remote_copy(
            src_ref=mine[a].at[rows, :],
            dst_ref=acts.at[a, g, rows, :],
            send_sem=x_send.at[a, g, half],
            recv_sem=x_recv.at[a, g, half],
            device_id=(left, right)[g],
            device_id_type=MESH,
        )

    def onward(a, g):
        rows = (low, high)[g]
        return pltpu.make_async_remote_copy(
            src_ref=acts.at[a, g, rows, :],
            dst_ref=acts.at[a, 2, rows, :],
            send_sem=f_send.at[a, g],
            recv_sem=f_recv.at[a, g],
            device_id=(left, right)[g],
            device_id_type=MESH,
        )

    for first in range(2):
        for a in range(2):
            for g in range(2):
                sideways(a, g, g if first == 0 else 1 - g).start()

    for a in range(2):
        acts[a, 3] = mine[a][...]
    in_acc[...] = jnp.zeros_like(in_acc)
    out_acc[...] = jnp.zeros_like(out_acc)

    def move(k, q, source, target_ref, target):
        return pltpu.make_async_remote_copy(
            src_ref=source,
            dst_ref=target_ref,
            send_sem=rs_send.at[q, k],
            recv_sem=rs_recv.at[q, k],
            device_id=target,
            device_id_type=MESH,
        )

    zp, zm, zz = (z + 1) % 4, (z + 3) % 4, (z + 2) % 4
    first16, last16 = pl.ds(0, 16), pl.ds(16, 16)

    def moves(q):
        return (
            move(0, q, part.at[q, :, :, 1 - c], paired.at[q], other),
            move(1, q, summed.at[q, :, zz, first16, :], hop1.at[q, 0], up),
            move(2, q, summed.at[q, :, zz, last16, :], hop1.at[q, 1], down),
            move(3, q, summed.at[q, :, zp], hop2.at[q, 0], up),
            move(4, q, summed.at[q, :, zm], hop2.at[q, 1], down),
            move(5, q, total.at[q, 1 - h], last.at[q], across),
        )

    def scatter0(q):
        weight(q).wait()
        value = dot(pre_error[...], win[q], 1, 1).astype(BF16)
        part[q] = value.reshape(2, 4, 2, TOK, W)
        moves(q)[0].start()

    def scatter1(q):
        m = moves(q)
        m[0].wait_recv()
        for hh in range(2):
            for zi in range(4):
                summed[q, hh, zi] = (
                    part[q, hh, zi, c].astype(F32) + paired[q, hh, zi].astype(F32)
                ).astype(BF16)
        m[1].start()
        m[2].start()

    def scatter2(q):
        m = moves(q)
        for k, row, rows in ((0, zp, first16), (1, zm, last16)):
            m[1 + k].wait_recv()
            for hh in range(2):
                summed[q, hh, row, rows, :] = (
                    summed[q, hh, row, rows, :].astype(F32)
                    + hop1[q, k, hh].astype(F32)
                ).astype(BF16)
            m[3 + k].start()

    def scatter3(q):
        m = moves(q)
        m[3].wait_recv()
        m[4].wait_recv()
        for hh in range(2):
            total[q, hh] = (
                summed[q, hh, z].astype(F32)
                + hop2[q, 0, hh].astype(F32)
                + hop2[q, 1, hh].astype(F32)
            ).astype(BF16)
        m[5].start()

    def scatter4(q):
        moves(q)[5].wait_recv()
        cols = pl.ds(pl.multiple_of(q * W, W), W)
        norm_error[:, cols] = total[q, h].astype(F32) + last[q].astype(F32)

    def unit(u, g, half):
        in_acc[half] += dot(all_normed[u], acts[0, g], 0, 0)
        out_acc[half] += dot(acts[1, g], all_errors[u], 0, 0)

    @pl.loop(0, PIECES + 4)
    def _(t):
        @pl.when(t < PIECES)
        def _():
            scatter0(t)

        @pl.when(t < 6)
        def _():
            gather.stage0(t, (slice_normed.at[t], slice_errors.at[t]))
            own = gather.rows(0, 0)
            all_normed[t, own, :] = slice_normed[t]
            all_errors[t, own, :] = slice_errors[t]

        @pl.when((t >= 1) & (t < PIECES + 1))
        def _():
            scatter1(t - 1)

        @pl.when((t >= 2) & (t < PIECES + 2))
        def _():
            scatter2(t - 2)

        @pl.when((t >= 1) & (t < 7))
        def _():
            gather.stage1(t - 1)

        @pl.when((t >= 3) & (t < PIECES + 3))
        def _():
            scatter3(t - 3)

        @pl.when((t >= 2) & (t < 8))
        def _():
            gather.stage2(t - 2)

        @pl.when(t >= 4)
        def _():
            scatter4(t - 4)

        @pl.when((t >= 3) & (t < 9))
        def _():
            gather.stage3(t - 3)

        @pl.when(t == 1)
        def _():
            for copy in loads:
                copy.wait()

        @pl.when(t == 5)
        def _():
            for a in range(2):
                for g in range(2):
                    sideways(a, g, g).wait_recv()
                    onward(a, g).start()

        @pl.when(t == 8)
        def _():
            for a in range(2):
                for g in range(2):
                    sideways(a, g, 1 - g).wait_recv()

        @pl.when(t == PIECES + 3)
        def _():
            for a in range(2):
                for g in range(2):
                    onward(a, g).wait_recv()

        @pl.when((t == 1) | (t == 2))
        def _():
            unit(t + 5, 3, t - 1)

        @pl.when(t >= 8)
        def _():
            gather.stage4(t - 8)
            unit(t - 8, (t - 8) // 2, (t - 8) % 2)

    for u in range(4, 6):
        gather.stage4(u)

    @pl.loop(4, 6)
    def _(u):
        unit(u, u // 2, u % 2)

    for half in range(2):
        in_grad[pl.ds(half * W, W), :] = in_acc[half].astype(BF16)
        out_grad[:, pl.ds(half * W, W)] = out_acc[half].astype(BF16)

    for a in range(2):
        for g in range(2):
            sideways(a, g, 0).wait_send()
            sideways(a, g, 1).wait_send()
            onward(a, g).wait_send()

    @pl.loop(0, 6)
    def _(p):
        gather.finish(p)

    @pl.loop(0, PIECES)
    def _(q):
        for m in moves(q):
            m.wait_send()


def shape(dims, dtype=BF16):
    return jax.ShapeDtypeStruct(dims, dtype)


VM = pl.BlockSpec(memory_space=pltpu.VMEM)
ANY = pl.BlockSpec(memory_space=pl.ANY)
DMA = pltpu.SemaphoreType.DMA


def forward_call(normed, errors, w_in, w_out):
    return pl.pallas_call(
        forward_kernel,
        name="forward",
        out_shape=(
            shape((GROUP, W)), shape((GROUP, W)),
            shape((2, GROUP, W)), shape((2, GROUP, W)),
            shape((6, TOK, W)), shape((6, TOK, W)),
        ),
        in_specs=[VM, VM, ANY, ANY],
        out_specs=(VM, VM, ANY, ANY, ANY, ANY),
        scratch_shapes=[
            pltpu.VMEM((PIECES, GROUP, W), BF16),
            pltpu.VMEM((PIECES, GROUP, W), BF16),
            pltpu.VMEM((PIECES, W, W), BF16),
            pltpu.VMEM((PIECES, W, W), BF16),
            pltpu.VMEM((GROUP, W), F32),
            pltpu.VMEM((GROUP, W), F32),
            *gather_scratch(PIECES),
            DMA((3, 2, 2)), DMA((3, 2, 2)), DMA((PIECES, 2)), DMA((2, 2)),
        ],
        compiler_params=pltpu.CompilerParams(
            collective_id=0, has_side_effects=True, vmem_limit_bytes=LIMIT
        ),
    )(normed, errors, w_in, w_out)


def backward_call(*args):
    return pl.pallas_call(
        backward_kernel,
        name="backward",
        out_shape=(
            shape((TOK, W * PIECES), F32), shape((2 * W, W)), shape((W, 2 * W)),
        ),
        in_specs=[VM, VM, ANY, ANY, VM, VM, ANY],
        out_specs=(VM, VM, VM),
        scratch_shapes=[
            pltpu.VMEM((8, GROUP, W), BF16),
            pltpu.VMEM((8, GROUP, W), BF16),
            pltpu.VMEM((2, 4, GROUP, W), BF16),
            pltpu.VMEM((PIECES, W, W), BF16),
            pltpu.VMEM((PIECES, 2, 4, 2, TOK, W), BF16),
            pltpu.VMEM((PIECES, 2, 4, TOK, W), BF16),
            pltpu.VMEM((PIECES, 2, 4, TOK, W), BF16),
            pltpu.VMEM((PIECES, 2, 2, 16, W), BF16),
            pltpu.VMEM((PIECES, 2, 2, TOK, W), BF16),
            pltpu.VMEM((PIECES, 2, TOK, W), BF16),
            pltpu.VMEM((PIECES, TOK, W), BF16),
            pltpu.VMEM((2, W, W), F32),
            pltpu.VMEM((2, W, W), F32),
            *gather_scratch(6),
            DMA((2, 2, 2)), DMA((2, 2, 2)), DMA((2, 2)), DMA((2, 2)),
            DMA((PIECES,)), DMA((2, 2)), DMA((PIECES, 6)), DMA((PIECES, 6)),
        ],
        compiler_params=pltpu.CompilerParams(
            collective_id=1, has_side_effects=True, vmem_limit_bytes=LIMIT
        ),
    )(*args)


def shifted(block, axis, distance):
    devices = range(lax.axis_size(axis))
    route = [((i - distance) % len(devices), i) for i in devices]
    return lax.ppermute(block, axis, route)


def per_device(features, delayed_error, ln_gain, w_in, w_out):
    errors = delayed_error[0]
    scale = ln_gain[0]
    in_block, out_block = w_in[0], w_out[0]
    values = features[0].astype(F32)
    average = jnp.mean(values, -1, keepdims=True)
    centred = values - average
    variance = jnp.mean(centred * centred, -1, keepdims=True)
    inverse = lax.rsqrt(variance + EPSILON)
    centred = centred * inverse
    normed = (centred * scale).astype(BF16)
    pre_error, active, own_n, own_e, slice_n, slice_e = forward_call(
        normed, errors, in_block, out_block
    )
    norm_error, in_total, out_total = backward_call(
        pre_error, active, own_n, own_e, slice_n, slice_e, in_block
    )
    scaled = norm_error * scale
    corrected = inverse * (
        scaled
        - jnp.mean(scaled, -1, keepdims=True)
        - centred * jnp.mean(scaled * centred, -1, keepdims=True)
    )
    own_error = (errors.astype(F32) + corrected).astype(BF16)
    gain_part = jnp.sum(norm_error * centred, 0)
    gain_grad = jnp.sum(lax.all_gather(gain_part, ("dp", "shard")), 0)
    passed = shifted(own_error, "section", -1)
    return passed[None], gain_grad[None], in_total[None], out_total[None]


def solution(mesh):
    return jax.shard_map(
        per_device,
        mesh=mesh,
        in_specs=(
            P("section", ("dp", "shard"), None),
            P("section", ("dp", "shard"), None),
            P("section", None),
            P("section", None, "shard"),
            P("section", "shard", None),
        ),
        out_specs=(
            P("section", ("dp", "shard"), None),
            P("section", None),
            P("section", "dp", "shard"),
            P("section", "shard", "dp"),
        ),
        check_vma=False,
    )
```

time: 595 us -> 235 us (0.39)
  blocking collectives: 333 us -> 0 us
  Pallas kernels: 0 us -> 141 us
  waiting for transfers between devices: 187 us -> 61.8 us
  matrix products: 51.4 us -> 0 us
  local copies, waits for them, and re-layouts: 0.76 us -> 7.09 us
    psum x1 -> x0, blocking collectives: 333 us -> none  [per_device(): gain_grad = lax.psum(jnp.sum(norm_error * centred, 0), ('dp', 'shard'))]
    pallas_call x0 -> x2, Pallas kernels: none -> 141 us  [the longest x1 77.4 us: backward_call(): pl.pallas_call(backward_kernel, name='backward', out_shape=(shape((TOK, W...]
    reduce_scatter x3 -> x0, waiting for transfers between devices: 66.3 us -> none  [the longest x1 66.3 us: per_device(): lax.psum_scatter(jnp.einsum('tf,df->td', pre_error, in_block, preferred_e...]
    all_gather x2 -> x1, waiting for transfers between devices: 120 us -> 54.6 us  [per_device(): gain_grad = jnp.sum(lax.all_gather(gain_part, ('dp', 'shard')), 0)]
    dot_general x5 -> x0, matrix products: 51.4 us -> none  [the longest x1 10.8 us: per_device(): jnp.einsum('tf,df->td', pre_error, in_block, preferred_element_type=jnp.f...]
    ppermute x1, waiting for transfers between devices: 0.01 us -> 7.18 us  [shifted(): return lax.ppermute(block, axis, route)]
  transfers between devices with their start and end apart: 6 -> 2, of which waited for: 3 -> 2; matrix products, arithmetic and copies ran while one was open for 6% -> 1% of each run, Pallas kernels for 0% -> 0%
where the time goes in v1:
time: 235 us; the launch traced here: 233 us
  Pallas kernels  141 us (60%)
  waiting for transfers between devices  61.8 us (26%)
  between operations  14.1 us (6%)
  other arithmetic  8.93 us (4%)
  local copies, waits for them, and re-layouts  7.09 us (3%)
    pallas_call x1, Pallas kernels, backward_call(): pl.pallas_call(backward_kernel, name='backward', out_shape=(shape((TOK, W...  77.4 us
    pallas_call x1, Pallas kernels, forward_call(): pl.pallas_call(forward_kernel, name='forward', out_shape=(shape((GROUP, W...  63.3 us
    all_gather x1, waiting for transfers between devices, per_device(): gain_grad = jnp.sum(lax.all_gather(gain_part, ('dp', 'shard')), 0)  54.6 us
    ppermute x1, waiting for transfers between devices, shifted(): return lax.ppermute(block, axis, route)  7.18 us
    unnamed x7, local copies, waits for them, and re-layouts  5.53 us
  transfers between devices with their start and end apart: 2, of which 2 were waited for; matrix products, arithmetic and copies ran while one was open for 1% of the time, Pallas kernels for 0%

profile of v1, /device:TPU:0, one launch (start us, length us, event | category | flops | bytes accessed | tf_op | source)
XLA Modules:
  0.0 233.4 jit_solution(13936318471209238411)
XLA Ops:
  7.2 0.0 all-gather.3.cloned.1.call-start
  7.2 1.2 convert_reduce_fusion
  8.4 1.3 fusion.14
  9.7 1.9 fusion.7.normed
  11.6 63.3 %forward.1 = (bf16[512,768]{1,0:T(8,128)(2,1)}, bf16[512,768]{1,0:T(8,128)(2,1)}, bf16[2,512,768]{2,1,0:T(8,128)(2,1)}, bf16[2,512,768]{2,1,0:T(8,128)(2,1)}, bf...) custom-call(bf16[32,6144]{1,0:T(8,128)(2,1)} %fusion.7.normed, bf16[32,6144]{1,0:T(8,128)(2,1)} %bitcast.46, ...), custom_call_target="tpu_custom_call" | custom-call | tf_op jit(solution)/shard_map/forward/pallas_call | solution.py:519
  74.9 0.0 copy-start.1
  74.9 77.4 %backward.1 = (f32[32,6144]{1,0:T(8,128)}, bf16[1536,768]{1,0:T(8,128)(2,1)}, bf16[768,1536]{1,0:T(8,128)(2,1)}) custom-call(bf16[512,768]{1,0:T(8,128)(2,1)} %get-tuple-element.13.pre_error, bf16[512,768]{1,0:T(8,128)(2,1)} %get-tuple-element.14.active, bf16[2,512,768]{2,1,0:T(8,128)(2,1)} %get-tuple-element.15.own_normed, ...), custom_call_target="tpu_custom_call" | custom-call | tf_op jit(solution)/shard_map/backward/pallas_call | solution.py:546
  152.3 0.0 copy-done.1
  152.4 2.2 fusion.13
  154.5 0.0 all-gather.3.cloned.1.call-update
  154.6 1.7 fusion.12
  156.2 0.7 collective-permute-start
  156.9 7.2 %collective-permute-done = bf16[32,6144]{1,0:T(8,128)(2,1)S(1)} collective-permute-done((bf16[32,6144]{1,0:T(8,128)(2,1)S(1)}, bf16[32,6144]{1,0:T(8,128)(2,1)S(1)}, u32[]{:S(2)}, u32[]{:S(2)}) %collective-permute-start) | collective-permute-done | bytes 393248 | tf_op jit(solution)/shard_map/ppermute | solution.py:581
  164.1 54.6 %all-gather.3.cloned.1.call-done = f32[393216]{0:T(1024)} async-done(((f32[6144]{0:T(1024)}), f32[393216]{0:T(1024)}) %all-gather.3.cloned.1.call-update) | async-done | bytes 1572880 | tf_op jit(solution)/shard_map/all_gather | solution.py:609
  218.7 1.6 reshape.29
  220.3 0.7 reduce_sum.59
  221.0 0.7 copy.12
  221.7 0.0 copy-start
  221.8 3.4 %copy.13 = bf16[1,1536,768]{2,1,0:T(8,128)(2,1)} copy(bf16[1,1536,768]{2,1,0:T(8,128)(2,1)} %bitcast.45) | data formatting | bytes 4718592
  225.1 0.0 copy-done
  225.1 1.4 copy.14
  (3 shorter events, 0.0 us)
Async XLA Ops:
  7.2 211.6 %all-gather.3.cloned.1.call-start = ((), (), s32[]{:S(2)}) async-start(), calls=%async_computation | async-start | bytes 1597440 | tf_op jit(solution)/shard_map/all_gather | solution.py:609
  74.9 77.5 %copy-start.1 = (f32[1,6144]{1,0:T(1,128)S(1)}, f32[1,6144]{1,0:T(1,128)}, u32[]{:S(2)}) copy-start(f32[1,6144]{1,0:T(1,128)} %param.7) | copy-start | bytes 73732
  156.2 7.9 %collective-permute-start = (bf16[32,6144]{1,0:T(8,128)(2,1)S(1)}, bf16[32,6144]{1,0:T(8,128)(2,1)S(1)}, u32[]{:S(2)}, u32[]{:S(2)}) collective-permute-start(bf16[32,6144]{1,0:T(8,128)(2,1)S(1)} %fusion.12), channel_id=1, source_target_pairs={{64,0},{0,64},{65,1},{1,65},{66,2},{2,66},{67,3},{3,67},{68,4},{4,... | collective-permute-start | bytes 1179656 | tf_op jit(solution)/shard_map/ppermute | solution.py:581
  221.7 3.4 %copy-start = (bf16[768,1536]{1,0:T(8,128)(2,1)S(1)}, bf16[768,1536]{1,0:T(8,128)(2,1)}, u32[]{:S(2)}) copy-start(bf16[768,1536]{1,0:T(8,128)(2,1)} %get-tuple-element.21) | copy-start | bytes 7077892
Sparse Core Ops, SparseCore 0:
  154.7 64.0 all-gather.2

commit v2 on v1

v2 whole, which is shorter than its diff:
```python
import functools

import jax
import jax.numpy as jnp
from jax import lax
from jax.experimental import pallas as pl
from jax.experimental.pallas import tpu as pltpu
from jax.sharding import PartitionSpec as P

SQRT_HALF = 0.7071067811865476
INV_ROOT_TWO_PI = 0.3989422804014327
EPSILON = 1e-06
F32 = jnp.float32
BF16 = jnp.bfloat16
MESH = pl.DeviceIdType.MESH
W = 768
TOK = 32
GROUP = 512
PIECES = 8
ALL = 14
LIMIT = 66_900_000

Y0, ZP, ZM, YZP, YZM, FA, FB, YFA, YFB = range(9)


def place():
    s = lax.axis_index("section")
    d = lax.axis_index("dp")
    j = lax.axis_index("shard")
    return s, d, j // 8, (j // 2) % 4, j % 2


def neighbour(dx=0, dh=0, dz=0, dc=0, ds=0):
    s, d, h, z, c = place()
    return (
        (s + ds) % 2,
        (d + dx + 4) % 4,
        ((h + dh) % 2) * 8 + ((z + dz + 4) % 4) * 2 + (c + dc) % 2,
    )


def greet(barrier, targets):
    for target in targets:
        pl.semaphore_signal(barrier, inc=1, device_id=target, device_id_type=MESH)
    pl.semaphore_wait(barrier, len(targets))


def dot(a, b, ca, cb):
    return lax.dot_general(
        a, b, (((ca,), (cb,)), ((), ())), preferred_element_type=F32
    )


class Gather:
    def __init__(self, bufs, send, recv, core_recv):
        self.bufs, self.send, self.recv, self.core_recv = bufs, send, recv, core_recv

    def rows(self, dh, dz, dc=0, first=0, count=TOK):
        _, _, h, z, c = place()
        block = ((h + dh) % 2) * 8 + ((z + dz + 4) % 4) * 2 + (c + dc) % 2
        return pl.ds(pl.multiple_of(block * TOK + first, 16), count)

    def copy(self, p, a, rows, sem, target, source=None):
        there = self.bufs[a].at[p, rows, :]
        return pltpu.make_async_remote_copy(
            src_ref=there if source is None else source,
            dst_ref=there,
            send_sem=self.send.at[p, a],
            recv_sem=sem,
            device_id=target,
            device_id_type=MESH,
        )

    def put(self, p, a, rows, kind, target, source=None):
        self.copy(p, a, rows, self.recv.at[p, a, kind], target, source).start()

    def got(self, p, a, rows, kind):
        self.copy(p, a, rows, self.recv.at[p, a, kind], neighbour(dz=1)).wait_recv()

    def to_core(self, p, a, dh, dz, source=None):
        rows = self.rows(dh, dz)
        sem = self.core_recv.at[p, a, dh * 4 + dz % 4]
        self.copy(p, a, rows, sem, neighbour(dc=1), source).start()

    def stage0(self, p, sources):
        up, down, across = neighbour(dz=1), neighbour(dz=-1), neighbour(dh=1)
        own = self.rows(0, 0)
        for a in range(2):
            self.put(p, a, own, Y0, across, sources[a])
            self.put(p, a, own, ZM, up, sources[a])
            self.put(p, a, own, ZP, down, sources[a])
            self.to_core(p, a, 0, 0, sources[a])

    def stage1(self, p):
        up, down, across = neighbour(dz=1), neighbour(dz=-1), neighbour(dh=1)
        self.got(p, 0, self.rows(1, 0), Y0)
        self.put(p, 0, self.rows(1, 0), YZM, up)
        self.put(p, 0, self.rows(1, 0), YZP, down)
        self.to_core(p, 0, 1, 0)
        for a in range(2):
            self.got(p, a, self.rows(0, 1), ZP)
            self.put(p, a, self.rows(0, 1, 0, 0, 16), FA, down)
            self.to_core(p, a, 0, 1)
            self.got(p, a, self.rows(0, -1), ZM)
            self.put(p, a, self.rows(0, -1, 0, 16, 16), FB, up)
            self.to_core(p, a, 0, -1)
        self.put(p, 1, self.rows(0, 1), YZP, across)
        self.put(p, 1, self.rows(0, -1), YZM, across)
        self.got(p, 1, self.rows(1, 0), Y0)
        self.to_core(p, 1, 1, 0)

    def stage2(self, p):
        up, down, across = neighbour(dz=1), neighbour(dz=-1), neighbour(dh=1)
        self.got(p, 0, self.rows(1, 1), YZP)
        self.put(p, 0, self.rows(1, 1, 0, 0, 16), YFA, down)
        self.to_core(p, 0, 1, 1)
        self.got(p, 0, self.rows(1, -1), YZM)
        self.put(p, 0, self.rows(1, -1, 0, 16, 16), YFB, up)
        self.to_core(p, 0, 1, -1)
        for a in (1, 0):
            self.got(p, a, self.rows(0, 2, 0, 0, 16), FA)
            self.got(p, a, self.rows(0, 2, 0, 16, 16), FB)
            if a == 1:
                self.put(p, 1, self.rows(0, 2), YFA, across)
            self.to_core(p, a, 0, 2)
        self.got(p, 1, self.rows(1, 1), YZP)
        self.to_core(p, 1, 1, 1)
        self.got(p, 1, self.rows(1, -1), YZM)
        self.to_core(p, 1, 1, -1)

    def stage3(self, p):
        self.got(p, 0, self.rows(1, 2, 0, 0, 16), YFA)
        self.got(p, 0, self.rows(1, 2, 0, 16, 16), YFB)
        self.to_core(p, 0, 1, 2)
        self.got(p, 1, self.rows(1, 2), YFA)
        self.to_core(p, 1, 1, 2)

    def stage4(self, p):
        for a in range(2):
            for dh in range(2):
                for dz in range(4):
                    rows = self.rows(dh, dz, 1)
                    sem = self.core_recv.at[p, a, dh * 4 + dz]
                    self.copy(p, a, rows, sem, neighbour(dc=1)).wait_recv()

    def finish(self, p):
        for a in range(2):
            part = self.bufs[a].at[p, pl.ds(0, 480), :]
            pltpu.make_async_copy(part, part, self.send.at[p, a]).wait()


def gather_scratch(pieces):
    return [
        pltpu.SemaphoreType.DMA((pieces, 2)),
        pltpu.SemaphoreType.DMA((pieces, 2, 9)),
        pltpu.SemaphoreType.DMA((pieces, 2, 8)),
    ]


def kernel(
    features, errors, gain, w_in, w_out,
    passed, gain_grad, in_grad, out_grad,
    all_normed, all_errors, acts, win, wout, part, paired, summed, hop1, hop2, total,
    last, in_acc, out_acc, staged, normed, centred, inverses, norm_error, own_error,
    slice_normed, slice_errors, gains,
    send, recv, core_recv, c_send, c_recv, x_send, x_recv, f_send, f_recv, w_sem,
    o_sem, rs_send, rs_recv, g_send, g_recv, p_send, p_recv,
):
    _, d, h, z, c = place()
    up, down, left, right = (
        neighbour(dz=1), neighbour(dz=-1), neighbour(dx=-1), neighbour(dx=1),
    )
    across, other, partner = neighbour(dh=1), neighbour(dc=1), neighbour(ds=1)

    def load_in(k):
        cols = pl.ds(pl.multiple_of(k % PIECES * W, W), W)
        return pltpu.make_async_copy(
            w_in.at[cols, :], win.at[k % 3], w_sem.at[0, k % 3]
        )

    def load_out(k):
        cols = pl.ds(pl.multiple_of(k * W, W), W)
        return pltpu.make_async_copy(
            w_out.at[:, cols], wout.at[k % 2], w_sem.at[1, k % 2]
        )

    for k in range(3):
        load_in(k).start()
    for k in range(2):
        load_out(k).start()

    scale = gain[...]
    for first in range(0, TOK, 16):
        rows = pl.ds(first, 16)
        values = features[rows, :].astype(F32)
        average = jnp.mean(values, -1, keepdims=True)
        values = values - average
        variance = jnp.mean(values * values, -1, keepdims=True)
        inverse = lax.rsqrt(variance + EPSILON)
        values = values * inverse
        centred[rows, :] = values
        inverses[rows, :] = jnp.broadcast_to(inverse, (16, 128))
        normed[rows, :] = (values * scale).astype(BF16)

    gather = Gather((all_normed, all_errors), send, recv, core_recv)
    greet(
        pltpu.get_barrier_semaphore(),
        [up, down, left, right, across, other, partner]
        + [neighbour(dz=2), neighbour(dx=2), neighbour(dh=1, dc=1)],
    )

    def crossing(g, half, a):
        dx = (-1, 1, 2)[g]
        cols = pl.ds(pl.multiple_of((((d + dx + 4) % 4) * 2 + half) * W, W), W)
        return pltpu.make_async_remote_copy(
            src_ref=(normed, errors)[a].at[:, cols],
            dst_ref=(slice_normed, slice_errors)[a].at[g * 2 + half],
            send_sem=c_send.at[g * 2 + half, a],
            recv_sem=c_recv.at[g * 2 + half, a],
            device_id=neighbour(dx=dx),
            device_id_type=MESH,
        )

    def stage0(p):
        cols = pl.ds(pl.multiple_of(p * W, W), W)
        gather.stage0(p, (normed.at[:, cols], errors.at[:, cols]))
        own = gather.rows(0, 0)
        all_normed[p, own, :] = normed[:, cols]
        all_errors[p, own, :] = errors[:, cols]

    def stage0_slice(p):
        u = p - PIECES
        for a, buf in enumerate((slice_normed, slice_errors)):
            pltpu.make_async_remote_copy(
                src_ref=buf.at[u],
                dst_ref=buf.at[u],
                send_sem=c_send.at[u, a],
                recv_sem=c_recv.at[u, a],
                device_id=right,
                device_id_type=MESH,
            ).wait_recv()
        gather.stage0(p, (slice_normed.at[u], slice_errors.at[u]))
        own = gather.rows(0, 0)
        all_normed[p, own, :] = slice_normed[u]
        all_errors[p, own, :] = slice_errors[u]

    @pl.loop(0, 12)
    def _(t):
        @pl.when(t < PIECES)
        def _():
            stage0(t)

        @pl.when(t == 0)
        def _():
            for g in range(3):
                for half in range(2):
                    for a in range(2):
                        crossing(g, half, a).start()

        @pl.when((t >= 1))
        def _():
            gather.stage1(t - 1)

        @pl.when((t >= 2))
        def _():
            gather.stage2(t - 2)

        @pl.when((t >= 3))
        def _():
            gather.stage3(t - 3)

        @pl.when(t >= PIECES)
        def _():
            stage0_slice(t)

        @pl.when(t >= 4)
        def _():
            p = t - 4
            gather.stage4(p)
            load_in(p).wait()
            load_out(p).wait()
            pre = dot(all_normed[p], win[p % 3], 1, 0)
            back = dot(all_errors[p], wout[p % 2], 1, 1)
            rows = pl.ds(0, GROUP)

            @pl.when(p == 0)
            def _():
                in_acc[0, rows, :] = pre
                in_acc[1, rows, :] = back

            @pl.when(p > 0)
            def _():
                in_acc[0, rows, :] += pre
                in_acc[1, rows, :] += back

            load_in(p + 3).start()

            @pl.when(p < PIECES - 2)
            def _():
                load_out(p + 2).start()

    @pl.loop(0, GROUP // 32)
    def _(i):
        rows = pl.ds(pl.multiple_of(i * 32, 32), 32)
        x = in_acc[0, rows, :]
        cdf = 0.5 * (1.0 + lax.erf(x * SQRT_HALF))
        density = INV_ROOT_TWO_PI * jnp.exp(-0.5 * x * x)
        acts[1, 3, rows, :] = (x * cdf).astype(BF16)
        acts[0, 3, rows, :] = (in_acc[1, rows, :] * (cdf + x * density)).astype(BF16)

    low, high = pl.ds(0, 256), pl.ds(256, 256)

    def sideways(a, g, half):
        rows = (low, high)[half]
        return pltpu.make_async_remote_copy(
            src_ref=acts.at[a, 3, rows, :],
            dst_ref=acts.at[a, g, rows, :],
            send_sem=x_send.at[a, g, half],
            recv_sem=x_recv.at[a, g, half],
            device_id=(left, right)[g],
            device_id_type=MESH,
        )

    def onward(a, g):
        rows = (low, high)[g]
        return pltpu.make_async_remote_copy(
            src_ref=acts.at[a, g, rows, :],
            dst_ref=acts.at[a, 2, rows, :],
            send_sem=f_send.at[a, g],
            recv_sem=f_recv.at[a, g],
            device_id=(left, right)[g],
            device_id_type=MESH,
        )

    for first in range(2):
        for a in range(2):
            for g in range(2):
                sideways(a, g, g if first == 0 else 1 - g).start()

    def move(k, q, source, target_ref, target):
        return pltpu.make_async_remote_copy(
            src_ref=source,
            dst_ref=target_ref,
            send_sem=rs_send.at[q, k],
            recv_sem=rs_recv.at[q, k],
            device_id=target,
            device_id_type=MESH,
        )

    zp, zm, zz = (z + 1) % 4, (z + 3) % 4, (z + 2) % 4
    first16, last16 = pl.ds(0, 16), pl.ds(16, 16)

    def m0(q):
        return move(0, q, part.at[q % 3, :, :, 1 - c], paired.at[q], other)

    def m1(q):
        return move(1, q, summed.at[q, :, zz, first16, :], hop1.at[q, 0], up)

    def m2(q):
        return move(2, q, summed.at[q, :, zz, last16, :], hop1.at[q, 1], down)

    def m3(q):
        return move(3, q, summed.at[q, :, zp], hop2.at[q, 0], up)

    def m4(q):
        return move(4, q, summed.at[q, :, zm], hop2.at[q, 1], down)

    def m5(q):
        return move(5, q, total.at[q, 1 - h], last.at[q], across)

    def scatter0(q):
        @pl.when(q >= 3)
        def _():
            m0(q - 3).wait_send()

        load_in(q + PIECES).wait()
        value = dot(acts[0, 3], win[(q + PIECES) % 3], 1, 1).astype(BF16)
        part[q % 3] = value.reshape(2, 4, 2, TOK, W)
        m0(q).start()

        @pl.when(q < PIECES - 3)
        def _():
            load_in(q + PIECES + 3).start()

    def scatter1(q):
        m0(q).wait_recv()
        for hh in range(2):
            for zi in range(4):
                summed[q, hh, zi] = (
                    part[q % 3, hh, zi, c].astype(F32) + paired[q, hh, zi].astype(F32)
                ).astype(BF16)
        m1(q).start()
        m2(q).start()

    def scatter2(q):
        for k, row, rows, came, go in (
            (0, zp, first16, m1, m3), (1, zm, last16, m2, m4),
        ):
            came(q).wait_recv()
            for hh in range(2):
                summed[q, hh, row, rows, :] = (
                    summed[q, hh, row, rows, :].astype(F32)
                    + hop1[q, k, hh].astype(F32)
                ).astype(BF16)
            go(q).start()

    def scatter3(q):
        m3(q).wait_recv()
        m4(q).wait_recv()
        for hh in range(2):
            total[q, hh] = (
                summed[q, hh, z].astype(F32)
                + hop2[q, 0, hh].astype(F32)
                + hop2[q, 1, hh].astype(F32)
            ).astype(BF16)
        m5(q).start()

    def scatter4(q):
        m5(q).wait_recv()
        cols = pl.ds(pl.multiple_of(q * W, W), W)
        norm_error[:, cols] = total[q, h].astype(F32) + last[q].astype(F32)

    def unit(u, g, half):
        gather.stage4(u)
        in_acc[half] += dot(all_normed[u], acts[0, g], 0, 0)
        out_acc[half] += dot(acts[1, g], all_errors[u], 0, 0)

    @pl.loop(12, PIECES + 16)
    def _(t):
        q = t - 12

        @pl.when(q < PIECES)
        def _():
            scatter0(q)

        @pl.when((q >= 1) & (q < PIECES + 1))
        def _():
            scatter1(q - 1)

        @pl.when((q >= 2) & (q < PIECES + 2))
        def _():
            scatter2(q - 2)

        @pl.when((q >= 3) & (q < PIECES + 3))
        def _():
            scatter3(q - 3)

        @pl.when(q >= 4)
        def _():
            scatter4(q - 4)

        @pl.when(t < ALL)
        def _():
            stage0_slice(t)

        @pl.when(t < ALL + 1)
        def _():
            gather.stage1(t - 1)

        @pl.when(t < ALL + 2)
        def _():
            gather.stage2(t - 2)

        @pl.when(t < ALL + 3)
        def _():
            gather.stage3(t - 3)

        @pl.when((q == 1) | (q == 2))
        def _():
            half = q - 1
            u = d * 2 + half
            in_acc[half] = dot(all_normed[u], acts[0, 3], 0, 0)
            out_acc[half] = dot(acts[1, 3], all_errors[u], 0, 0)

        @pl.when(q == 5)
        def _():
            for a in range(2):
                for g in range(2):
                    sideways(a, g, g).wait_recv()
                    onward(a, g).start()

        @pl.when(q == 8)
        def _():
            for a in range(2):
                for g in range(2):
                    sideways(a, g, 1 - g).wait_recv()

        @pl.when(q >= 8)
        def _():
            unit(q, (q - 8) // 2, q % 2)

    for q in range(PIECES):
        cols = pl.ds(q * W, W)
        product = norm_error[:, cols] * centred[:, cols]
        mine = jnp.sum(product, 0, keepdims=True)
        gains[0, h * 2 + c, pl.ds(q, 1), :] = mine

    def spread(level, k):
        target, slot = (
            ((neighbour(dc=1), neighbour(dh=1), neighbour(dh=1, dc=1))[k], h * 2 + c),
            (neighbour(dz=k + 1), z),
            (neighbour(dx=k + 1), d),
        )[level]
        return pltpu.make_async_remote_copy(
            src_ref=gains.at[level, slot],
            dst_ref=gains.at[level, slot],
            send_sem=g_send.at[level, k],
            recv_sem=g_recv.at[level, k],
            device_id=target,
            device_id_type=MESH,
        )

    def collect(level):
        for k in range(3):
            spread(level, k).wait_recv()
        value = gains[level, 0] + gains[level, 1] + gains[level, 2] + gains[level, 3]
        if level == 2:
            gain_grad[...] = value
            return
        gains[level + 1, (z, d)[level]] = value
        for k in range(3):
            spread(level + 1, k).start()

    for k in range(3):
        spread(0, k).start()

    for first in range(0, TOK, 16):
        rows = pl.ds(first, 16)
        scaled = norm_error[rows, :] * scale
        around = centred[rows, :]
        shift = jnp.mean(scaled, -1, keepdims=True)
        slope = jnp.mean(scaled * around, -1, keepdims=True)
        corrected = inverses[rows, pl.ds(0, 1)] * (scaled - shift - around * slope)
        own_error[rows, :] = (errors[rows, :].astype(F32) + corrected).astype(BF16)
    swap = pltpu.make_async_remote_copy(
        src_ref=own_error,
        dst_ref=passed,
        send_sem=p_send,
        recv_sem=p_recv,
        device_id=partner,
        device_id_type=MESH,
    )
    swap.start()

    for a in range(2):
        for g in range(2):
            onward(a, g).wait_recv()

    def emit(half):
        part_of = pl.ds(pl.multiple_of(half * W, W), W)
        return (
            pltpu.make_async_copy(staged.at[0], in_grad.at[part_of, :], o_sem.at[0]),
            pltpu.make_async_copy(staged.at[1], out_grad.at[:, part_of], o_sem.at[1]),
        )

    @pl.loop(0, 2)
    def _(half):
        unit(12 + half, 2, half)

        @pl.when(half == 1)
        def _():
            for copy in emit(0):
                copy.wait()

        staged[0] = in_acc[half].astype(BF16)
        staged[1] = out_acc[half].astype(BF16)
        for copy in emit(half):
            copy.start()

        @pl.when(half == 0)
        def _():
            collect(0)

        @pl.when(half == 1)
        def _():
            collect(1)

    for g in range(3):
        for half in range(2):
            for a in range(2):
                crossing(g, half, a).wait_send()
    for a in range(2):
        for g in range(2):
            sideways(a, g, 0).wait_send()
            sideways(a, g, 1).wait_send()
            onward(a, g).wait_send()

    @pl.loop(0, ALL)
    def _(p):
        gather.finish(p)

    @pl.loop(0, PIECES)
    def _(q):
        @pl.when(q >= PIECES - 3)
        def _():
            m0(q).wait_send()

        for m in (m1, m2, m3, m4, m5):
            m(q).wait_send()

    collect(2)
    for level in range(3):
        for k in range(3):
            spread(level, k).wait_send()
    swap.wait()
    for copy in emit(1):
        copy.wait()


def shape(dims, dtype=BF16):
    return jax.ShapeDtypeStruct(dims, dtype)


VM = pl.BlockSpec(memory_space=pltpu.VMEM)
ANY = pl.BlockSpec(memory_space=pl.ANY)
DMA = pltpu.SemaphoreType.DMA


def block_call(features, errors, gain, w_in, w_out):
    bf16, f32 = functools.partial(pltpu.VMEM, dtype=BF16), functools.partial(
        pltpu.VMEM, dtype=F32
    )
    return pl.pallas_call(
        kernel,
        name="block",
        out_shape=(
            shape((TOK, W * PIECES)), shape((8, W), F32),
            shape((2 * W, W)), shape((W, 2 * W)),
        ),
        in_specs=[VM, VM, VM, ANY, ANY],
        out_specs=(ANY, VM, ANY, ANY),
        scratch_shapes=[
            bf16((ALL, GROUP, W)),
            bf16((ALL, GROUP, W)),
            bf16((2, 4, GROUP, W)),
            bf16((3, W, W)),
            bf16((2, W, W)),
            bf16((3, 2, 4, 2, TOK, W)),
            bf16((PIECES, 2, 4, TOK, W)),
            bf16((PIECES, 2, 4, TOK, W)),
            bf16((PIECES, 2, 2, 16, W)),
            bf16((PIECES, 2, 2, TOK, W)),
            bf16((PIECES, 2, TOK, W)),
            bf16((PIECES, TOK, W)),
            f32((2, W, W)),
            f32((2, W, W)),
            bf16((2, W, W)),
            bf16((TOK, W * PIECES)),
            f32((TOK, W * PIECES)),
            f32((TOK, 128)),
            f32((TOK, W * PIECES)),
            bf16((TOK, W * PIECES)),
            bf16((6, TOK, W)),
            bf16((6, TOK, W)),
            f32((3, 4, 8, W)),
            *gather_scratch(ALL),
            DMA((6, 2)), DMA((6, 2)), DMA((2, 2, 2)), DMA((2, 2, 2)),
            DMA((2, 2)), DMA((2, 2)), DMA((2, 3)), DMA((2,)),
            DMA((PIECES, 6)), DMA((PIECES, 6)), DMA((3, 3)), DMA((3, 3)),
            DMA, DMA,
        ],
        compiler_params=pltpu.CompilerParams(
            collective_id=0, has_side_effects=True, vmem_limit_bytes=LIMIT
        ),
    )(features, errors, gain, w_in, w_out)


def per_device(features, delayed_error, ln_gain, w_in, w_out):
    passed, gain_grad, in_total, out_total = block_call(
        features[0], delayed_error[0], ln_gain, w_in[0], w_out[0]
    )
    return passed[None], gain_grad.reshape(1, -1), in_total[None], out_total[None]


def solution(mesh):
    return jax.shard_map(
        per_device,
        mesh=mesh,
        in_specs=(
            P("section", ("dp", "shard"), None),
            P("section", ("dp", "shard"), None),
            P("section", None),
            P("section", None, "shard"),
            P("section", "shard", None),
        ),
        out_specs=(
            P("section", ("dp", "shard"), None),
            P("section", None),
            P("section", "dp", "shard"),
            P("section", "shard", "dp"),
        ),
        check_vma=False,
    )
```

time: 235 us -> 148 us (0.63)
  waiting for transfers between devices: 61.8 us -> 0 us
  between operations: 14.1 us -> 0.64 us
  other arithmetic: 8.93 us -> 0 us
    all_gather x1 -> x0, waiting for transfers between devices: 54.6 us -> none  [per_device(): gain_grad = jnp.sum(lax.all_gather(gain_part, ('dp', 'shard')), 0)]
    ppermute x1 -> x0, waiting for transfers between devices: 7.18 us -> none  [shifted(): return lax.ppermute(block, axis, route)]
    reduce_sum x4 -> x0, other arithmetic: 5.3 us -> none  [the longest x1 2.16 us: per_device(): gain_part = jnp.sum(norm_error * centred, 0)]
    convert_element_type x2 -> x0, other arithmetic: 3.62 us -> none  [the longest x1 1.93 us: per_device(): normed = (centred * scale).astype(BF16)]
    unnamed x7 -> x6, local copies, waits for them, and re-layouts: 5.53 us -> 7.92 us
    pallas_call x2 -> x1, Pallas kernels: 141 us -> 139 us  [block_call(): pl.pallas_call(kernel, name='block', out_shape=(shape((TOK, W * PIECES)),...]
  transfers between devices with their start and end apart: 2 -> 0, of which waited for: 2 -> 0; matrix products, arithmetic and copies ran while one was open for 1% -> 0% of each run, Pallas kernels for 0% -> 0%
where the time goes in v2:
time: 148 us
  Pallas kernels  139 us (94%)
  local copies, waits for them, and re-layouts  7.92 us (5%)
    pallas_call x1, Pallas kernels, block_call(): pl.pallas_call(kernel, name='block', out_shape=(shape((TOK, W * PIECES)),...  139 us
    unnamed x6, local copies, waits for them, and re-layouts  7.92 us

profile of v2, /device:TPU:0, one launch (start us, length us, event | category | flops | bytes accessed | tf_op | source)
XLA Modules:
  0.0 147.8 jit_solution(4790758493237801684)
XLA Ops:
  0.6 139.3 %block.1 = (bf16[32,6144]{1,0:T(8,128)(2,1)}, f32[8,768]{1,0:T(8,128)}, bf16[1536,768]{1,0:T(8,128)(2,1)}, bf16[768,1536]{1,0:T(8,128)(2,1)}) custom-call(bf16[32,6144]{1,0:T(8,128)(2,1)} %bitcast.15, bf16[32,6144]{1,0:T(8,128)(2,1)} %bitcast.16, f32[1,6144]{1,0:T(1,128)} %gain.1, bf16[6144,768]{1,0:T(8,128)(2,1)} %bitcast.10, bf16[768,6144]{1,0:T(8,128)(2,1)} %bitcast.11), custom_call_target="tpu_custom_call" | custom-call | tf_op jit(solution)/shard_map/block/pallas_call | solution.py:623
  139.9 1.4 copy.9
  141.3 1.8 %copy.13 = bf16[1,32,6144]{2,1,0:T(8,128)(2,1)} copy(bf16[1,32,6144]{2,1,0:T(8,128)(2,1)} %bitcast.14) | data formatting | bytes 786432
  143.1 0.0 copy-start
  143.1 3.4 %copy.14 = bf16[1,1536,768]{2,1,0:T(8,128)(2,1)} copy(bf16[1,1536,768]{2,1,0:T(8,128)(2,1)} %bitcast.13) | data formatting | bytes 4718592
  146.4 0.0 copy-done
  146.4 1.4 copy.15
Async XLA Ops:
  143.1 3.4 %copy-start = (bf16[768,1536]{1,0:T(8,128)(2,1)S(1)}, bf16[768,1536]{1,0:T(8,128)(2,1)}, u32[]{:S(2)}) copy-start(bf16[768,1536]{1,0:T(8,128)(2,1)} %get-tuple-element.11) | copy-start | bytes 7077892

commit v3 on v2

v3 whole, which is shorter than its diff:
```python
import functools

import jax
import jax.numpy as jnp
from jax import lax
from jax.experimental import pallas as pl
from jax.experimental.pallas import tpu as pltpu
from jax.sharding import PartitionSpec as P

SQRT_HALF = 0.7071067811865476
INV_ROOT_TWO_PI = 0.3989422804014327
EPSILON = 1e-06
F32 = jnp.float32
BF16 = jnp.bfloat16
MESH = pl.DeviceIdType.MESH
W = 768
WIDE = 2 * W
HALF = 16
TOK = 32
GROUP = 512
PIECES = 8
ALL = 14
LIMIT = 66_900_000

Y0, ZP, ZM, YZP, YZM, FA, FB, YFA, YFB = range(9)


def place():
    s = lax.axis_index("section")
    d = lax.axis_index("dp")
    j = lax.axis_index("shard")
    return s, d, j // 8, (j // 2) % 4, j % 2


def neighbour(dx=0, dh=0, dz=0, dc=0, ds=0):
    s, d, h, z, c = place()
    return (
        (s + ds) % 2,
        (d + dx + 4) % 4,
        ((h + dh) % 2) * 8 + ((z + dz + 4) % 4) * 2 + (c + dc) % 2,
    )


def greet(barrier, targets):
    for target in targets:
        pl.semaphore_signal(barrier, inc=1, device_id=target, device_id_type=MESH)
    pl.semaphore_wait(barrier, len(targets))


def dot(a, b, ca, cb):
    return lax.dot_general(
        a, b, (((ca,), (cb,)), ((), ())), preferred_element_type=F32
    )


FULL, LEFT, RIGHT = pl.ds(0, WIDE), pl.ds(0, W), pl.ds(W, W)


class Gather:
    def __init__(self, bufs, send, recv, core_recv):
        self.bufs, self.send, self.recv, self.core_recv = bufs, send, recv, core_recv

    def block(self, dh, dz, dc=0):
        _, _, h, z, c = place()
        index = ((h + dh) % 2) * 8 + ((z + dz + 4) % 4) * 2 + (c + dc) % 2
        return pl.ds(pl.multiple_of(index * HALF, HALF), HALF)

    def copy(self, p, a, rows, sem, target, source=None, cols=FULL):
        there = self.bufs[a].at[p, rows, cols]
        return pltpu.make_async_remote_copy(
            src_ref=there if source is None else source,
            dst_ref=there,
            send_sem=self.send.at[p, a],
            recv_sem=sem,
            device_id=target,
            device_id_type=MESH,
        )

    def put(self, p, a, rows, kind, target, source=None, cols=FULL):
        sem = self.recv.at[p, a, kind]
        self.copy(p, a, rows, sem, target, source, cols).start()

    def got(self, p, a, rows, kind, cols=FULL):
        sem = self.recv.at[p, a, kind]
        self.copy(p, a, rows, sem, neighbour(dz=1), None, cols).wait_recv()

    def to_core(self, p, a, dh, dz, source=None):
        sem = self.core_recv.at[p, a, dh * 4 + dz % 4]
        self.copy(p, a, self.block(dh, dz), sem, neighbour(dc=1), source).start()

    def stage0(self, p, sources):
        up, down, across = neighbour(dz=1), neighbour(dz=-1), neighbour(dh=1)
        own = self.block(0, 0)
        for a in range(2):
            self.put(p, a, own, Y0, across, sources[a])
            self.put(p, a, own, ZM, up, sources[a])
            self.put(p, a, own, ZP, down, sources[a])
            self.to_core(p, a, 0, 0, sources[a])

    def stage1(self, p):
        up, down, across = neighbour(dz=1), neighbour(dz=-1), neighbour(dh=1)
        self.got(p, 0, self.block(1, 0), Y0)
        self.put(p, 0, self.block(1, 0), YZM, up)
        self.put(p, 0, self.block(1, 0), YZP, down)
        self.to_core(p, 0, 1, 0)
        for a in range(2):
            self.got(p, a, self.block(0, 1), ZP)
            self.put(p, a, self.block(0, 1), FA, down, None, LEFT)
            self.to_core(p, a, 0, 1)
            self.got(p, a, self.block(0, -1), ZM)
            self.put(p, a, self.block(0, -1), FB, up, None, RIGHT)
            self.to_core(p, a, 0, -1)
        self.put(p, 1, self.block(0, 1), YZP, across)
        self.put(p, 1, self.block(0, -1), YZM, across)
        self.got(p, 1, self.block(1, 0), Y0)
        self.to_core(p, 1, 1, 0)

    def stage2(self, p):
        up, down, across = neighbour(dz=1), neighbour(dz=-1), neighbour(dh=1)
        self.got(p, 0, self.block(1, 1), YZP)
        self.put(p, 0, self.block(1, 1), YFA, down, None, LEFT)
        self.to_core(p, 0, 1, 1)
        self.got(p, 0, self.block(1, -1), YZM)
        self.put(p, 0, self.block(1, -1), YFB, up, None, RIGHT)
        self.to_core(p, 0, 1, -1)
        for a in (1, 0):
            self.got(p, a, self.block(0, 2), FA, LEFT)
            self.got(p, a, self.block(0, 2), FB, RIGHT)
            if a == 1:
                self.put(p, 1, self.block(0, 2), YFA, across)
            self.to_core(p, a, 0, 2)
        self.got(p, 1, self.block(1, 1), YZP)
        self.to_core(p, 1, 1, 1)
        self.got(p, 1, self.block(1, -1), YZM)
        self.to_core(p, 1, 1, -1)

    def stage3(self, p):
        self.got(p, 0, self.block(1, 2), YFA, LEFT)
        self.got(p, 0, self.block(1, 2), YFB, RIGHT)
        self.to_core(p, 0, 1, 2)
        self.got(p, 1, self.block(1, 2), YFA)
        self.to_core(p, 1, 1, 2)

    def stage4(self, p):
        for a in range(2):
            for dh in range(2):
                for dz in range(4):
                    rows = self.block(dh, dz, 1)
                    sem = self.core_recv.at[p, a, dh * 4 + dz]
                    self.copy(p, a, rows, sem, neighbour(dc=1)).wait_recv()

    def finish(self, p):
        for a in range(2):
            part = self.bufs[a].at[p, pl.ds(0, 15 * HALF), :]
            pltpu.make_async_copy(part, part, self.send.at[p, a]).wait()


def gather_scratch(pieces):
    return [
        pltpu.SemaphoreType.DMA((pieces, 2)),
        pltpu.SemaphoreType.DMA((pieces, 2, 9)),
        pltpu.SemaphoreType.DMA((pieces, 2, 8)),
    ]


def kernel(
    features, errors, gain, w_in, w_out,
    passed, gain_grad, in_grad, out_grad,
    all_normed, all_errors, acts, win, wout, part, paired, summed, hop1, hop2, total,
    last, in_acc, out_acc, normed, centred, inverses, norm_error, own_error,
    slice_normed, slice_errors, gains,
    send, recv, core_recv, c_send, c_recv, x_send, x_recv, f_send, f_recv, w_sem,
    o_sem, rs_send, rs_recv, g_send, g_recv, p_send, p_recv,
):
    _, d, h, z, c = place()
    up, down, left, right = (
        neighbour(dz=1), neighbour(dz=-1), neighbour(dx=-1), neighbour(dx=1),
    )
    across, other, partner = neighbour(dh=1), neighbour(dc=1), neighbour(ds=1)

    def load_in(k):
        cols = pl.ds(pl.multiple_of(k % 8 * W, W), W)
        return pltpu.make_async_copy(
            w_in.at[cols, :], win.at[k % 3], w_sem.at[0, k % 3]
        )

    def load_out(k):
        cols = pl.ds(pl.multiple_of(k % 8 * W, W), W)
        return pltpu.make_async_copy(
            w_out.at[:, cols], wout.at[k % 2], w_sem.at[1, k % 2]
        )

    for k in range(3):
        load_in(k).start()
    for k in range(2):
        load_out(k).start()

    scale = gain[...]
    for first in range(0, TOK, 16):
        rows = pl.ds(first, 16)
        values = features[rows, :].astype(F32)
        average = jnp.mean(values, -1, keepdims=True)
        values = values - average
        variance = jnp.mean(values * values, -1, keepdims=True)
        inverse = lax.rsqrt(variance + EPSILON)
        values = values * inverse
        centred[rows, :] = values
        inverses[rows, :] = jnp.broadcast_to(inverse, (16, 128))
        normed[rows, :] = (values * scale).astype(BF16)

    gather = Gather((all_normed, all_errors), send, recv, core_recv)
    greet(
        pltpu.get_barrier_semaphore(),
        [up, down, left, right, across, other, partner]
        + [neighbour(dz=2), neighbour(dx=2), neighbour(dh=1, dc=1)],
    )

    def tokens(tau):
        return pl.ds(pl.multiple_of(tau * HALF, HALF), HALF)

    def crossing(g, tau, a):
        dx = (-1, 1, 2)[g]
        cols = pl.ds(pl.multiple_of((d + dx + 4) % 4 * WIDE, WIDE), WIDE)
        return pltpu.make_async_remote_copy(
            src_ref=(normed, errors)[a].at[tokens(tau), cols],
            dst_ref=(slice_normed, slice_errors)[a].at[tau * 3 + g],
            send_sem=c_send.at[tau * 3 + g, a],
            recv_sem=c_recv.at[tau * 3 + g, a],
            device_id=neighbour(dx=dx),
            device_id_type=MESH,
        )

    def stage0(p):
        rows = tokens(p // 4)
        cols = pl.ds(pl.multiple_of(p % 4 * WIDE, WIDE), WIDE)
        gather.stage0(p, (normed.at[rows, cols], errors.at[rows, cols]))
        own = gather.block(0, 0)
        all_normed[p, own, :] = normed[rows, cols]
        all_errors[p, own, :] = errors[rows, cols]

    def stage0_slice(p):
        u = p - PIECES
        for a, buf in enumerate((slice_normed, slice_errors)):
            pltpu.make_async_remote_copy(
                src_ref=buf.at[u],
                dst_ref=buf.at[u],
                send_sem=c_send.at[u, a],
                recv_sem=c_recv.at[u, a],
                device_id=right,
                device_id_type=MESH,
            ).wait_recv()
        gather.stage0(p, (slice_normed.at[u], slice_errors.at[u]))
        own = gather.block(0, 0)
        all_normed[p, own, :] = slice_normed[u]
        all_errors[p, own, :] = slice_errors[u]

    def acting(tau):
        return pl.ds(pl.multiple_of(tau * 256, 256), 256)

    def activate(tau):
        @pl.loop(0, 8)
        def _(i):
            rows = pl.ds(pl.multiple_of(tau * 256 + i * 32, 32), 32)
            x = in_acc[0, rows, :]
            cdf = 0.5 * (1.0 + lax.erf(x * SQRT_HALF))
            density = INV_ROOT_TWO_PI * jnp.exp(-0.5 * x * x)
            acts[1, 3, rows, :] = (x * cdf).astype(BF16)
            acts[0, 3, rows, :] = (in_acc[1, rows, :] * (cdf + x * density)).astype(
                BF16
            )

    def sideways(tau, a, g, part_of):
        rows = pl.ds(pl.multiple_of(tau * 256 + part_of * 128, 128), 128)
        return pltpu.make_async_remote_copy(
            src_ref=acts.at[a, 3, rows, :],
            dst_ref=acts.at[a, g, rows, :],
            send_sem=x_send.at[tau, a, g, part_of],
            recv_sem=x_recv.at[tau, a, g, part_of],
            device_id=(left, right)[g],
            device_id_type=MESH,
        )

    def onward(tau, a, g):
        rows = pl.ds(pl.multiple_of(tau * 256 + g * 128, 128), 128)
        return pltpu.make_async_remote_copy(
            src_ref=acts.at[a, g, rows, :],
            dst_ref=acts.at[a, 2, rows, :],
            send_sem=f_send.at[tau, a, g],
            recv_sem=f_recv.at[tau, a, g],
            device_id=(left, right)[g],
            device_id_type=MESH,
        )

    def each(act):
        for a in range(2):
            for g in range(2):
                act(a, g)

    def move(k, q, source, target_ref, target):
        return pltpu.make_async_remote_copy(
            src_ref=source,
            dst_ref=target_ref,
            send_sem=rs_send.at[q, k],
            recv_sem=rs_recv.at[q, k],
            device_id=target,
            device_id_type=MESH,
        )

    zp, zm, zz = (z + 1) % 4, (z + 3) % 4, (z + 2) % 4

    def m0(q):
        return move(0, q, part.at[q % 3, :, :, 1 - c], paired.at[q], other)

    def m1(q):
        return move(1, q, summed.at[q, :, zz, :, LEFT], hop1.at[q, 0], up)

    def m2(q):
        return move(2, q, summed.at[q, :, zz, :, RIGHT], hop1.at[q, 1], down)

    def m3(q):
        return move(3, q, summed.at[q, :, zp], hop2.at[q, 0], up)

    def m4(q):
        return move(4, q, summed.at[q, :, zm], hop2.at[q, 1], down)

    def m5(q):
        return move(5, q, total.at[q, 1 - h], last.at[q], across)

    def scatter1(q):
        m0(q).wait_recv()
        for hh in range(2):
            for zi in range(4):
                summed[q, hh, zi] = (
                    part[q % 3, hh, zi, c].astype(F32) + paired[q, hh, zi].astype(F32)
                ).astype(BF16)
        m1(q).start()
        m2(q).start()

    def scatter2(q):
        for k, row, cols, came, go in (
            (0, zp, LEFT, m1, m3), (1, zm, RIGHT, m2, m4),
        ):
            came(q).wait_recv()
            for hh in range(2):
                summed[q, hh, row, :, cols] = (
                    summed[q, hh, row, :, cols].astype(F32)
                    + hop1[q, k, hh].astype(F32)
                ).astype(BF16)
            go(q).start()

    def scatter3(q):
        m3(q).wait_recv()
        m4(q).wait_recv()
        for hh in range(2):
            total[q, hh] = (
                summed[q, hh, z].astype(F32)
                + hop2[q, 0, hh].astype(F32)
                + hop2[q, 1, hh].astype(F32)
            ).astype(BF16)
        m5(q).start()

    def scatter4(q):
        m5(q).wait_recv()
        cols = pl.ds(pl.multiple_of(q % 4 * WIDE, WIDE), WIDE)
        norm_error[tokens(q // 4), cols] = total[q, h].astype(F32) + last[q].astype(F32)

    def products(u, g, tau, half):
        cols = (LEFT, RIGHT)[half] if isinstance(half, int) else pl.ds(
            pl.multiple_of(half * W, W), W
        )
        rows = acting(tau)
        return (
            dot(all_normed[u, :, cols], acts[0, g, rows, :], 0, 0),
            dot(acts[1, g, rows, :], all_errors[u, :, cols], 0, 0),
        )

    def add_products(u, g, tau, half):
        to_in, to_out = products(u, g, tau, half)
        in_acc[half] += to_in
        out_acc[half] += to_out

    def correct(tau):
        rows = tokens(tau)
        scaled = norm_error[rows, :] * scale
        around = centred[rows, :]
        shift = jnp.mean(scaled, -1, keepdims=True)
        slope = jnp.mean(scaled * around, -1, keepdims=True)
        corrected = inverses[rows, pl.ds(0, 1)] * (scaled - shift - around * slope)
        own_error[rows, :] = (errors[rows, :].astype(F32) + corrected).astype(BF16)
        swap(tau).start()

    def swap(tau):
        return pltpu.make_async_remote_copy(
            src_ref=own_error.at[tokens(tau), :],
            dst_ref=passed.at[tokens(tau), :],
            send_sem=p_send.at[tau],
            recv_sem=p_recv.at[tau],
            device_id=partner,
            device_id_type=MESH,
        )

    def spread(level, k):
        target, slot = (
            ((neighbour(dc=1), neighbour(dh=1), neighbour(dh=1, dc=1))[k], h * 2 + c),
            (neighbour(dz=k + 1), z),
            (neighbour(dx=k + 1), d),
        )[level]
        return pltpu.make_async_remote_copy(
            src_ref=gains.at[level, slot],
            dst_ref=gains.at[level, slot],
            send_sem=g_send.at[level, k],
            recv_sem=g_recv.at[level, k],
            device_id=target,
            device_id_type=MESH,
        )

    def collect(level):
        for k in range(3):
            spread(level, k).wait_recv()
        value = gains[level, 0] + gains[level, 1] + gains[level, 2] + gains[level, 3]
        if level == 2:
            gain_grad[...] = value
            return
        gains[level + 1, (z, d)[level]] = value
        for k in range(3):
            spread(level + 1, k).start()

    def start_gain():
        for q in range(PIECES):
            cols = pl.ds(q * W, W)
            product = norm_error[:, cols] * centred[:, cols]
            mine = jnp.sum(product, 0, keepdims=True)
            gains[0, h * 2 + c, pl.ds(q, 1), :] = mine
        for k in range(3):
            spread(0, k).start()

    @pl.loop(0, 21)
    def _(t):
        @pl.when((t == 8) | (t == 12))
        def _():
            tau = t // 4 - 2
            activate(tau)
            each(lambda a, g: sideways(tau, a, g, g).start())
            each(lambda a, g: sideways(tau, a, g, 1 - g).start())

        @pl.when(t < PIECES)
        def _():
            stage0(t)

        @pl.when(t == 0)
        def _():
            for tau in range(2):
                for g in range(3):
                    for a in range(2):
                        crossing(g, tau, a).start()

        @pl.when((t >= 1) & (t < PIECES + 1))
        def _():
            gather.stage1(t - 1)

        @pl.when((t >= 2) & (t < PIECES + 2))
        def _():
            gather.stage2(t - 2)

        @pl.when((t >= 3) & (t < PIECES + 3))
        def _():
            gather.stage3(t - 3)

        @pl.when((t >= 4) & (t < PIECES + 4))
        def _():
            gather.stage4(t - 4)

        @pl.when(t >= 11)
        def _():
            @pl.when(t < 16)
            def _():
                m0(t - 11).wait_send()

        @pl.when((t >= 4) & (t < 16))
        def _():
            @pl.loop(0, 2)
            def _(half):
                k = (t - 4) * 2 + half
                cols = pl.ds(pl.multiple_of(half * W, W), W)
                load_in(k).wait()

                @pl.when(t < PIECES + 4)
                def _():
                    p = t - 4
                    load_out(k).wait()
                    pre = dot(all_normed[p, :, cols], win[k % 3], 1, 0)
                    back = dot(all_errors[p, :, cols], wout[k % 2], 1, 1)
                    rows = acting(p // 4)

                    @pl.when(k % 8 == 0)
                    def _():
                        in_acc[0, rows, :] = pre
                        in_acc[1, rows, :] = back

                    @pl.when(k % 8 > 0)
                    def _():
                        in_acc[0, rows, :] += pre
                        in_acc[1, rows, :] += back

                    @pl.when(k < 14)
                    def _():
                        load_out(k + 2).start()

                @pl.when(t >= 8)
                def _():
                    q = t - 8
                    known = acts[0, 3, acting(q // 4), :]
                    value = dot(known, win[k % 3], 1, 1).astype(BF16)
                    part[q % 3, :, :, :, :, cols] = value.reshape(2, 4, 2, HALF, W)

                @pl.when(k < 21)
                def _():
                    load_in(k + 3).start()

            @pl.when(t >= 8)
            def _():
                m0(t - 8).start()

        @pl.when((t >= 9) & (t < 17))
        def _():
            scatter1(t - 9)

        @pl.when((t >= 10) & (t < 18))
        def _():
            scatter2(t - 10)

        @pl.when((t >= 11) & (t < 19))
        def _():
            scatter3(t - 11)

        @pl.when((t >= 12) & (t < 20))
        def _():
            scatter4(t - 12)

        @pl.when(((t >= 9) & (t < 12)) | ((t >= 14) & (t < 17)))
        def _():
            stage0_slice(t - 1 - 2 * (t // 13))

        @pl.when(((t >= 10) & (t < 13)) | ((t >= 16) & (t < 19)))
        def _():
            gather.stage1(t - 2 - 3 * (t // 16))

        @pl.when(((t >= 11) & (t < 14)) | ((t >= 17) & (t < 20)))
        def _():
            gather.stage2(t - 3 - 3 * (t // 17))

        @pl.when(((t >= 12) & (t < 15)) | (t >= 18))
        def _():
            gather.stage3(t - 4 - 3 * (t // 18))

        @pl.when((t == 10) | (t == 14))
        def _():
            tau = (t - 10) // 4
            each(lambda a, g: sideways(tau, a, g, g).wait_recv())
            each(lambda a, g: onward(tau, a, g).start())

        @pl.when((t == 14) | (t == 18))
        def _():
            tau = (t - 14) // 4
            each(lambda a, g: sideways(tau, a, g, 1 - g).wait_recv())

        @pl.when(t == 16)
        def _():
            each(lambda a, g: onward(0, a, g).wait_recv())
            correct(0)

        @pl.when((t == 12) | (t == 13))
        def _():
            tau = t - 12

            @pl.loop(0, 2)
            def _(half):
                to_in, to_out = products(tau * 4 + d, 3, tau, half)

                @pl.when(tau == 0)
                def _():
                    in_acc[half] = to_in
                    out_acc[half] = to_out

                @pl.when(tau == 1)
                def _():
                    in_acc[half] += to_in
                    out_acc[half] += to_out

        @pl.when(t == 19)
        def _():
            start_gain()
            correct(1)

        @pl.when(t == 20)
        def _():
            collect(0)

        @pl.when(((t >= 15) & (t < 18)) | (t >= 19))
        def _():
            u = t - 15 - t // 19
            gather.stage4(PIECES + u)

            @pl.loop(0, 2)
            def _(half):
                add_products(PIECES + u, u % 3, u // 3, half)

    each(lambda a, g: onward(1, a, g).wait_recv())
    gather.stage4(13)

    def emit(half):
        part_of = pl.ds(pl.multiple_of(half * W, W), W)
        return (
            pltpu.make_async_copy(win.at[0], in_grad.at[part_of, :], o_sem.at[0]),
            pltpu.make_async_copy(win.at[1], out_grad.at[:, part_of], o_sem.at[1]),
        )

    @pl.loop(0, 2)
    def _(half):
        add_products(13, 2, 1, half)

        @pl.when(half == 1)
        def _():
            for copy in emit(0):
                copy.wait()

        win[0] = in_acc[half].astype(BF16)
        win[1] = out_acc[half].astype(BF16)
        for copy in emit(half):
            copy.start()

        @pl.when(half == 0)
        def _():
            collect(1)

    for tau in range(2):
        for g in range(3):
            for a in range(2):
                crossing(g, tau, a).wait_send()
        each(lambda a, g: sideways(tau, a, g, 0).wait_send())
        each(lambda a, g: sideways(tau, a, g, 1).wait_send())
        each(lambda a, g: onward(tau, a, g).wait_send())

    @pl.loop(0, ALL)
    def _(p):
        gather.finish(p)

    @pl.loop(0, PIECES)
    def _(q):
        @pl.when(q >= 5)
        def _():
            m0(q).wait_send()

        for m in (m1, m2, m3, m4, m5):
            m(q).wait_send()

    collect(2)
    for level in range(3):
        for k in range(3):
            spread(level, k).wait_send()
    for tau in range(2):
        swap(tau).wait()
    for copy in emit(1):
        copy.wait()


def shape(dims, dtype=BF16):
    return jax.ShapeDtypeStruct(dims, dtype)


VM = pl.BlockSpec(memory_space=pltpu.VMEM)
ANY = pl.BlockSpec(memory_space=pl.ANY)
DMA = pltpu.SemaphoreType.DMA


def block_call(features, errors, gain, w_in, w_out):
    bf16, f32 = functools.partial(pltpu.VMEM, dtype=BF16), functools.partial(
        pltpu.VMEM, dtype=F32
    )
    return pl.pallas_call(
        kernel,
        name="block",
        out_shape=(
            shape((TOK, W * PIECES)), shape((8, W), F32),
            shape((2 * W, W)), shape((W, 2 * W)),
        ),
        in_specs=[VM, VM, VM, ANY, ANY],
        out_specs=(ANY, VM, ANY, ANY),
        scratch_shapes=[
            bf16((ALL, 16 * HALF, WIDE)),
            bf16((ALL, 16 * HALF, WIDE)),
            bf16((2, 4, GROUP, W)),
            bf16((3, W, W)),
            bf16((2, W, W)),
            bf16((3, 2, 4, 2, HALF, WIDE)),
            bf16((PIECES, 2, 4, HALF, WIDE)),
            bf16((PIECES, 2, 4, HALF, WIDE)),
            bf16((PIECES, 2, 2, HALF, W)),
            bf16((PIECES, 2, 2, HALF, WIDE)),
            bf16((PIECES, 2, HALF, WIDE)),
            bf16((PIECES, HALF, WIDE)),
            f32((2, W, W)),
            f32((2, W, W)),
            bf16((TOK, W * PIECES)),
            f32((TOK, W * PIECES)),
            f32((TOK, 128)),
            f32((TOK, W * PIECES)),
            bf16((TOK, W * PIECES)),
            bf16((6, HALF, WIDE)),
            bf16((6, HALF, WIDE)),
            f32((3, 4, 8, W)),
            *gather_scratch(ALL),
            DMA((6, 2)), DMA((6, 2)), DMA((2, 2, 2, 2)), DMA((2, 2, 2, 2)),
            DMA((2, 2, 2)), DMA((2, 2, 2)), DMA((2, 3)), DMA((2,)),
            DMA((PIECES, 6)), DMA((PIECES, 6)), DMA((3, 3)), DMA((3, 3)),
            DMA((2,)), DMA((2,)),
        ],
        compiler_params=pltpu.CompilerParams(
            collective_id=0, has_side_effects=True, vmem_limit_bytes=LIMIT
        ),
    )(features, errors, gain, w_in, w_out)


def emit_kernel(
    passed, gain, in_grad, out_grad,
    passed_out, gain_out, in_out, out_out,
    a, b, load, save,
):
    pairs = []
    for k in range(4):
        rows = pl.ds(k * 384, 384)
        pairs.append((in_grad.at[rows, :], a.at[rows, :], in_out.at[rows, :]))
        rows = pl.ds(k * 192, 192)
        pairs.append((out_grad.at[rows, :], b.at[rows, :], out_out.at[rows, :]))
    pairs.append((passed, passed_out, None))
    loads = [
        pltpu.make_async_copy(source, held, load.at[k])
        for k, (source, held, _) in enumerate(pairs)
    ]
    for copy in loads:
        copy.start()
    for q in range(PIECES):
        gain_out[:, pl.ds(q * W, W)] = gain[pl.ds(q, 1), :]
    saves = []
    for k, (_, held, out) in enumerate(pairs):
        loads[k].wait()
        if out is not None:
            saves.append(pltpu.make_async_copy(held, out, save.at[k]))
            saves[-1].start()
    for copy in saves:
        copy.wait()


def emit_call(*results):
    return pl.pallas_call(
        emit_kernel,
        name="emit",
        out_shape=(
            shape((TOK, W * PIECES)), shape((1, W * PIECES), F32),
            shape((2 * W, W)), shape((W, 2 * W)),
        ),
        in_specs=[ANY, VM, ANY, ANY],
        out_specs=(VM, VM, ANY, ANY),
        scratch_shapes=[
            pltpu.VMEM((WIDE, W), BF16), pltpu.VMEM((W, WIDE), BF16),
            DMA((9,)), DMA((9,)),
        ],
    )(*results)


def per_device(features, delayed_error, ln_gain, w_in, w_out):
    results = block_call(features[0], delayed_error[0], ln_gain, w_in[0], w_out[0])
    passed, gain_grad, in_total, out_total = emit_call(*results)
    return passed[None], gain_grad, in_total[None], out_total[None]


def solution(mesh):
    return jax.shard_map(
        per_device,
        mesh=mesh,
        in_specs=(
            P("section", ("dp", "shard"), None),
            P("section", ("dp", "shard"), None),
            P("section", None),
            P("section", None, "shard"),
            P("section", "shard", None),
        ),
        out_specs=(
            P("section", ("dp", "shard"), None),
            P("section", None),
            P("section", "dp", "shard"),
            P("section", "shard", "dp"),
        ),
        check_vma=False,
    )
```

time: 148 us -> 141 us (0.953)
  local copies, waits for them, and re-layouts: 7.92 us -> 0 us
    unnamed x6 -> x0, local copies, waits for them, and re-layouts: 7.92 us -> none
    pallas_call x0 -> x1, Pallas kernels: none -> 5.62 us  [emit_call(): pl.pallas_call(emit_kernel, name='emit', out_shape=(shape((TOK, W * PIECE...]
    pallas_call x1, Pallas kernels: 139 us -> 135 us  [block_call(): pl.pallas_call(kernel, name='block', out_shape=(shape((TOK, W * PIECES)),...]
where the time goes in v3:
time: 141 us
  Pallas kernels  140 us (99%)
    pallas_call x1, Pallas kernels, block_call(): pl.pallas_call(kernel, name='block', out_shape=(shape((TOK, W * PIECES)),...  135 us
    pallas_call x1, Pallas kernels, emit_call(): pl.pallas_call(emit_kernel, name='emit', out_shape=(shape((TOK, W * PIECE...  5.62 us

profile of v3, /device:TPU:0, one launch (start us, length us, event | category | flops | bytes accessed | tf_op | source)
XLA Modules:
  0.0 141.1 jit_solution(16319569733861730447)
XLA Ops:
  0.6 134.8 %block.1 = (bf16[32,6144]{1,0:T(8,128)(2,1)}, f32[8,768]{1,0:T(8,128)}, bf16[1536,768]{1,0:T(8,128)(2,1)}, bf16[768,1536]{1,0:T(8,128)(2,1)}) custom-call(bf16[32,6144]{1,0:T(8,128)(2,1)} %bitcast.9, bf16[32,6144]{1,0:T(8,128)(2,1)} %bitcast.10, f32[1,6144]{1,0:T(1,128)} %gain.1, bf16[6144,768]{1,0:T(8,128)(2,1)} %bitcast.7, bf16[768,6144]{1,0:T(8,128)(2,1)} %bitcast.8), custom_call_target="tpu_custom_call" | custom-call | tf_op jit(solution)/shard_map/block/pallas_call | solution.py:680
  135.4 5.6 %emit.1 = (bf16[32,6144]{1,0:T(8,128)(2,1)}, f32[1,6144]{1,0:T(1,128)}, bf16[1536,768]{1,0:T(8,128)(2,1)}, bf16[768,1536]{1,0:T(8,128)(2,1)}) custom-call(bf16[32,6144]{1,0:T(8,128)(2,1)} %get-tuple-element.12.passed, f32[8,768]{1,0:T(8,128)} %get-tuple-element.13.gain, bf16[1536,768]{1,0:T(8,128)(2,1)} %get-tuple-element.14.in_grad, ...), custom_call_target="tpu_custom_call" | custom-call | tf_op jit(solution)/shard_map/emit/pallas_call | solution.py:755

commit v4 on v3

--- a/solution.py
+++ b/solution.py
@@ -22,9 +22,6 @@
 ALL = 14
 LIMIT = 66_900_000
 
-Y0, ZP, ZM, YZP, YZM, FA, FB, YFA, YFB = range(9)
-
-
 def place():
     s = lax.axis_index("section")
     d = lax.axis_index("dp")
@@ -76,78 +73,67 @@
             device_id_type=MESH,
         )
 
-    def put(self, p, a, rows, kind, target, source=None, cols=FULL):
-        sem = self.recv.at[p, a, kind]
+    def put(self, stage, p, a, rows, target, source=None, cols=FULL):
+        sem = self.recv.at[p, a, stage]
         self.copy(p, a, rows, sem, target, source, cols).start()
 
-    def got(self, p, a, rows, kind, cols=FULL):
-        sem = self.recv.at[p, a, kind]
-        self.copy(p, a, rows, sem, neighbour(dz=1), None, cols).wait_recv()
+    def got(self, stage, p, a):
+        rows = pl.ds(0, (3, 3, 1)[stage] * HALF)
+        sem = self.recv.at[p, a, stage]
+        self.copy(p, a, rows, sem, neighbour(dz=1)).wait_recv()
 
     def to_core(self, p, a, dh, dz, source=None):
-        sem = self.core_recv.at[p, a, dh * 4 + dz % 4]
+        sem = self.core_recv.at[p, a]
         self.copy(p, a, self.block(dh, dz), sem, neighbour(dc=1), source).start()
 
     def stage0(self, p, sources):
         up, down, across = neighbour(dz=1), neighbour(dz=-1), neighbour(dh=1)
         own = self.block(0, 0)
         for a in range(2):
-            self.put(p, a, own, Y0, across, sources[a])
-            self.put(p, a, own, ZM, up, sources[a])
-            self.put(p, a, own, ZP, down, sources[a])
+            self.put(0, p, a, own, across, sources[a])
+            self.put(0, p, a, own, up, sources[a])
+            self.put(0, p, a, own, down, sources[a])
             self.to_core(p, a, 0, 0, sources[a])
 
     def stage1(self, p):
         up, down, across = neighbour(dz=1), neighbour(dz=-1), neighbour(dh=1)
-        self.got(p, 0, self.block(1, 0), Y0)
-        self.put(p, 0, self.block(1, 0), YZM, up)
-        self.put(p, 0, self.block(1, 0), YZP, down)
-        self.to_core(p, 0, 1, 0)
         for a in range(2):
-            self.got(p, a, self.block(0, 1), ZP)
-            self.put(p, a, self.block(0, 1), FA, down, None, LEFT)
+            self.got(0, p, a)
+            if a == 0:
+                self.put(1, p, 0, self.block(1, 0), up)
+                self.put(1, p, 0, self.block(1, 0), down)
+            else:
+                self.put(1, p, 1, self.block(0, 1), across)
+                self.put(1, p, 1, self.block(0, -1), across)
+            self.put(1, p, a, self.block(0, 1), down, None, LEFT)
+            self.put(1, p, a, self.block(0, -1), up, None, RIGHT)
+            self.to_core(p, a, 1, 0)
             self.to_core(p, a, 0, 1)
-            self.got(p, a, self.block(0, -1), ZM)
-            self.put(p, a, self.block(0, -1), FB, up, None, RIGHT)
             self.to_core(p, a, 0, -1)
-        self.put(p, 1, self.block(0, 1), YZP, across)
-        self.put(p, 1, self.block(0, -1), YZM, across)
-        self.got(p, 1, self.block(1, 0), Y0)
-        self.to_core(p, 1, 1, 0)
 
     def stage2(self, p):
         up, down, across = neighbour(dz=1), neighbour(dz=-1), neighbour(dh=1)
-        self.got(p, 0, self.block(1, 1), YZP)
-        self.put(p, 0, self.block(1, 1), YFA, down, None, LEFT)
-        self.to_core(p, 0, 1, 1)
-        self.got(p, 0, self.block(1, -1), YZM)
-        self.put(p, 0, self.block(1, -1), YFB, up, None, RIGHT)
-        self.to_core(p, 0, 1, -1)
-        for a in (1, 0):
-            self.got(p, a, self.block(0, 2), FA, LEFT)
-            self.got(p, a, self.block(0, 2), FB, RIGHT)
-            if a == 1:
-                self.put(p, 1, self.block(0, 2), YFA, across)
+        for a in range(2):
+            self.got(1, p, a)
+            if a == 0:
+                self.put(2, p, 0, self.block(1, 1), down, None, LEFT)
+                self.put(2, p, 0, self.block(1, -1), up, None, RIGHT)
+            else:
+                self.put(2, p, 1, self.block(0, 2), across)
+            self.to_core(p, a, 1, 1)
+            self.to_core(p, a, 1, -1)
             self.to_core(p, a, 0, 2)
-        self.got(p, 1, self.block(1, 1), YZP)
-        self.to_core(p, 1, 1, 1)
-        self.got(p, 1, self.block(1, -1), YZM)
-        self.to_core(p, 1, 1, -1)
 
     def stage3(self, p):
-        self.got(p, 0, self.block(1, 2), YFA, LEFT)
-        self.got(p, 0, self.block(1, 2), YFB, RIGHT)
-        self.to_core(p, 0, 1, 2)
-        self.got(p, 1, self.block(1, 2), YFA)
-        self.to_core(p, 1, 1, 2)
+        for a in range(2):
+            self.got(2, p, a)
+            self.to_core(p, a, 1, 2)
 
     def stage4(self, p):
         for a in range(2):
-            for dh in range(2):
-                for dz in range(4):
-                    rows = self.block(dh, dz, 1)
-                    sem = self.core_recv.at[p, a, dh * 4 + dz]
-                    self.copy(p, a, rows, sem, neighbour(dc=1)).wait_recv()
+            rows = pl.ds(0, 8 * HALF)
+            sem = self.core_recv.at[p, a]
+            self.copy(p, a, rows, sem, neighbour(dc=1)).wait_recv()
 
     def finish(self, p):
         for a in range(2):
@@ -158,8 +144,8 @@
 def gather_scratch(pieces):
     return [
         pltpu.SemaphoreType.DMA((pieces, 2)),
-        pltpu.SemaphoreType.DMA((pieces, 2, 9)),
-        pltpu.SemaphoreType.DMA((pieces, 2, 8)),
+        pltpu.SemaphoreType.DMA((pieces, 2, 3)),
+        pltpu.SemaphoreType.DMA((pieces, 2)),
     ]
 
 
@@ -169,7 +155,7 @@
     all_normed, all_errors, acts, win, wout, part, paired, summed, hop1, hop2, total,
     last, in_acc, out_acc, normed, centred, inverses, norm_error, own_error,
     slice_normed, slice_errors, gains,
-    send, recv, core_recv, c_send, c_recv, x_send, x_recv, f_send, f_recv, w_sem,
+    send, recv, core_recv, c_send, c_recv, x_send, x_recv, w_sem,
     o_sem, rs_send, rs_recv, g_send, g_recv, p_send, p_recv,
 ):
     _, d, h, z, c = place()
@@ -178,14 +164,17 @@
     )
     across, other, partner = neighbour(dh=1), neighbour(dc=1), neighbour(ds=1)
 
+    def turn(p):
+        return (p + d + 1) % 4
+
     def load_in(k):
-        cols = pl.ds(pl.multiple_of(k % 8 * W, W), W)
+        cols = pl.ds(pl.multiple_of(turn(k // 2) * WIDE + k % 2 * W, W), W)
         return pltpu.make_async_copy(
             w_in.at[cols, :], win.at[k % 3], w_sem.at[0, k % 3]
         )
 
     def load_out(k):
-        cols = pl.ds(pl.multiple_of(k % 8 * W, W), W)
+        cols = pl.ds(pl.multiple_of(turn(k // 2) * WIDE + k % 2 * W, W), W)
         return pltpu.make_async_copy(
             w_out.at[:, cols], wout.at[k % 2], w_sem.at[1, k % 2]
         )
@@ -224,7 +213,7 @@
         return pltpu.make_async_remote_copy(
             src_ref=(normed, errors)[a].at[tokens(tau), cols],
             dst_ref=(slice_normed, slice_errors)[a].at[tau * 3 + g],
-            send_sem=c_send.at[tau * 3 + g, a],
+            send_sem=c_send,
             recv_sem=c_recv.at[tau * 3 + g, a],
             device_id=neighbour(dx=dx),
             device_id_type=MESH,
@@ -232,7 +221,7 @@
 
     def stage0(p):
         rows = tokens(p // 4)
-        cols = pl.ds(pl.multiple_of(p % 4 * WIDE, WIDE), WIDE)
+        cols = pl.ds(pl.multiple_of(turn(p) * WIDE, WIDE), WIDE)
         gather.stage0(p, (normed.at[rows, cols], errors.at[rows, cols]))
         own = gather.block(0, 0)
         all_normed[p, own, :] = normed[rows, cols]
@@ -244,7 +233,7 @@
             pltpu.make_async_remote_copy(
                 src_ref=buf.at[u],
                 dst_ref=buf.at[u],
-                send_sem=c_send.at[u, a],
+                send_sem=c_send,
                 recv_sem=c_recv.at[u, a],
                 device_id=right,
                 device_id_type=MESH,
@@ -253,6 +242,36 @@
         own = gather.block(0, 0)
         all_normed[p, own, :] = slice_normed[u]
         all_errors[p, own, :] = slice_errors[u]
+
+    def hand(p, g, act):
+        for a, buf in enumerate((all_normed, all_errors)):
+            for i in range(8):
+                rows = pl.ds(pl.multiple_of((i * 2 + c) * HALF, HALF), HALF)
+                act(
+                    pltpu.make_async_remote_copy(
+                        src_ref=buf.at[p, rows, :],
+                        dst_ref=buf.at[PIECES + g, rows, :],
+                        send_sem=send.at[PIECES + g, a],
+                        recv_sem=recv.at[PIECES + g, a, 0],
+                        device_id=(left, right)[g],
+                        device_id_type=MESH,
+                    )
+                )
+
+    def handed(g):
+        for a, buf in enumerate((all_normed, all_errors)):
+            there = buf.at[PIECES + g, pl.ds(0, 8 * HALF), :]
+            pltpu.make_async_copy(there, there, recv.at[PIECES + g, a, 0]).wait()
+            for i in range(8):
+                rows = pl.ds(pl.multiple_of((i * 2 + c) * HALF, HALF), HALF)
+                pltpu.make_async_remote_copy(
+                    src_ref=buf.at[PIECES + g, rows, :],
+                    dst_ref=buf.at[PIECES + g, rows, :],
+                    send_sem=send.at[PIECES + g, a],
+                    recv_sem=core_recv.at[PIECES + g, a],
+                    device_id=other,
+                    device_id_type=MESH,
+                ).start()
 
     def acting(tau):
         return pl.ds(pl.multiple_of(tau * 256, 256), 256)
@@ -274,8 +293,8 @@
         return pltpu.make_async_remote_copy(
             src_ref=acts.at[a, 3, rows, :],
             dst_ref=acts.at[a, g, rows, :],
-            send_sem=x_send.at[tau, a, g, part_of],
-            recv_sem=x_recv.at[tau, a, g, part_of],
+            send_sem=x_send.at[tau],
+            recv_sem=x_recv.at[tau, (part_of + g) % 2],
             device_id=(left, right)[g],
             device_id_type=MESH,
         )
@@ -285,11 +304,15 @@
         return pltpu.make_async_remote_copy(
             src_ref=acts.at[a, g, rows, :],
             dst_ref=acts.at[a, 2, rows, :],
-            send_sem=f_send.at[tau, a, g],
-            recv_sem=f_recv.at[tau, a, g],
+            send_sem=x_send.at[tau],
+            recv_sem=x_recv.at[tau, 2],
             device_id=(left, right)[g],
             device_id_type=MESH,
         )
+
+    def arrived(tau, k):
+        there = acts.at[0, 0]
+        pltpu.make_async_copy(there, there, x_recv.at[tau, k]).wait()
 
     def each(act):
         for a in range(2):
@@ -300,8 +323,8 @@
         return pltpu.make_async_remote_copy(
             src_ref=source,
             dst_ref=target_ref,
-            send_sem=rs_send.at[q, k],
-            recv_sem=rs_recv.at[q, k],
+            send_sem=rs_send.at[q, min(k, 1)],
+            recv_sem=rs_recv.at[q, (k + 1) // 2],
             device_id=target,
             device_id_type=MESH,
         )
@@ -336,11 +359,13 @@
         m1(q).start()
         m2(q).start()
 
+    def both(q, k, count):
+        there = hop2.at[q, pl.ds(0, count)]
+        pltpu.make_async_copy(there, there, rs_recv.at[q, k]).wait()
+
     def scatter2(q):
-        for k, row, cols, came, go in (
-            (0, zp, LEFT, m1, m3), (1, zm, RIGHT, m2, m4),
-        ):
-            came(q).wait_recv()
+        both(q, 1, 1)
+        for k, row, cols, go in ((0, zp, LEFT, m3), (1, zm, RIGHT, m4)):
             for hh in range(2):
                 summed[q, hh, row, :, cols] = (
                     summed[q, hh, row, :, cols].astype(F32)
@@ -349,8 +374,7 @@
             go(q).start()
 
     def scatter3(q):
-        m3(q).wait_recv()
-        m4(q).wait_recv()
+        both(q, 2, 2)
         for hh in range(2):
             total[q, hh] = (
                 summed[q, hh, z].astype(F32)
@@ -361,7 +385,7 @@
 
     def scatter4(q):
         m5(q).wait_recv()
-        cols = pl.ds(pl.multiple_of(q % 4 * WIDE, WIDE), WIDE)
+        cols = pl.ds(pl.multiple_of(turn(q) * WIDE, WIDE), WIDE)
         norm_error[tokens(q // 4), cols] = total[q, h].astype(F32) + last[q].astype(F32)
 
     def products(u, g, tau, half):
@@ -408,18 +432,19 @@
         return pltpu.make_async_remote_copy(
             src_ref=gains.at[level, slot],
             dst_ref=gains.at[level, slot],
-            send_sem=g_send.at[level, k],
-            recv_sem=g_recv.at[level, k],
+            send_sem=g_send.at[level],
+            recv_sem=g_recv.at[level],
             device_id=target,
             device_id_type=MESH,
         )
 
     def collect(level):
-        for k in range(3):
-            spread(level, k).wait_recv()
+        there = gains.at[level, pl.ds(0, 3)]
+        pltpu.make_async_copy(there, there, g_recv.at[level]).wait()
         value = gains[level, 0] + gains[level, 1] + gains[level, 2] + gains[level, 3]
         if level == 2:
-            gain_grad[...] = value
+            for q in range(PIECES):
+                gain_grad[:, pl.ds(q * W, W)] = value[q : q + 1, :]
             return
         gains[level + 1, (z, d)[level]] = value
         for k in range(3):
@@ -434,7 +459,7 @@
         for k in range(3):
             spread(0, k).start()
 
-    @pl.loop(0, 21)
+    @pl.loop(0, 20)
     def _(t):
         @pl.when((t == 8) | (t == 12))
         def _():
@@ -449,10 +474,9 @@
 
         @pl.when(t == 0)
         def _():
-            for tau in range(2):
-                for g in range(3):
-                    for a in range(2):
-                        crossing(g, tau, a).start()
+            for tau, g in ((0, 2), (1, 0), (1, 1), (1, 2)):
+                for a in range(2):
+                    crossing(g, tau, a).start()
 
         @pl.when((t >= 1) & (t < PIECES + 1))
         def _():
@@ -469,6 +493,14 @@
         @pl.when((t >= 4) & (t < PIECES + 4))
         def _():
             gather.stage4(t - 4)
+
+        @pl.when(t == 4)
+        def _():
+            hand(0, 1, lambda copy: copy.start())
+
+        @pl.when(t == 6)
+        def _():
+            hand(2, 0, lambda copy: copy.start())
 
         @pl.when(t >= 11)
         def _():
@@ -537,36 +569,44 @@
         def _():
             scatter4(t - 12)
 
-        @pl.when(((t >= 9) & (t < 12)) | ((t >= 14) & (t < 17)))
-        def _():
-            stage0_slice(t - 1 - 2 * (t // 13))
-
-        @pl.when(((t >= 10) & (t < 13)) | ((t >= 16) & (t < 19)))
-        def _():
-            gather.stage1(t - 2 - 3 * (t // 16))
-
-        @pl.when(((t >= 11) & (t < 14)) | ((t >= 17) & (t < 20)))
-        def _():
-            gather.stage2(t - 3 - 3 * (t // 17))
-
-        @pl.when(((t >= 12) & (t < 15)) | (t >= 18))
-        def _():
-            gather.stage3(t - 4 - 3 * (t // 18))
-
-        @pl.when((t == 10) | (t == 14))
-        def _():
-            tau = (t - 10) // 4
-            each(lambda a, g: sideways(tau, a, g, g).wait_recv())
+        @pl.when((t == 9) | ((t >= 13) & (t < 16)))
+        def _():
+            stage0_slice(t + 1 - 3 * (t // 13))
+
+        @pl.when((t == 10) | ((t >= 15) & (t < 18)))
+        def _():
+            gather.stage1(t - 4 * (t // 15))
+
+        @pl.when((t == 11) | ((t >= 16) & (t < 19)))
+        def _():
+            gather.stage2(t - 1 - 4 * (t // 16))
+
+        @pl.when((t == 12) | (t >= 17))
+        def _():
+            gather.stage3(t - 2 - 4 * (t // 17))
+
+        @pl.when(t == 10)
+        def _():
+            handed(1)
+
+        @pl.when(t == 12)
+        def _():
+            handed(0)
+
+        @pl.when((t == 12) | (t == 15))
+        def _():
+            tau = (t - 12) // 3
+            arrived(tau, 0)
             each(lambda a, g: onward(tau, a, g).start())
 
         @pl.when((t == 14) | (t == 18))
         def _():
             tau = (t - 14) // 4
-            each(lambda a, g: sideways(tau, a, g, 1 - g).wait_recv())
+            arrived(tau, 1)
 
         @pl.when(t == 16)
         def _():
-            each(lambda a, g: onward(0, a, g).wait_recv())
+            arrived(0, 2)
             correct(0)
 
         @pl.when((t == 12) | (t == 13))
@@ -575,7 +615,7 @@
 
             @pl.loop(0, 2)
             def _(half):
-                to_in, to_out = products(tau * 4 + d, 3, tau, half)
+                to_in, to_out = products(tau * 4 + 3, 3, tau, half)
 
                 @pl.when(tau == 0)
                 def _():
@@ -592,20 +632,17 @@
             start_gain()
             correct(1)
 
-        @pl.when(t == 20)
-        def _():
-            collect(0)
-
-        @pl.when(((t >= 15) & (t < 18)) | (t >= 19))
-        def _():
-            u = t - 15 - t // 19
+        @pl.when(t >= 15)
+        def _():
+            u = t - 15
             gather.stage4(PIECES + u)
 
             @pl.loop(0, 2)
             def _(half):
                 add_products(PIECES + u, u % 3, u // 3, half)
 
-    each(lambda a, g: onward(1, a, g).wait_recv())
+    collect(0)
+    arrived(1, 2)
     gather.stage4(13)
 
     def emit(half):
@@ -633,17 +670,23 @@
         def _():
             collect(1)
 
+    part_of = all_normed.at[0, pl.ds(0, 8 * HALF), :]
+    pltpu.make_async_copy(part_of, part_of, c_send).wait()
     for tau in range(2):
-        for g in range(3):
-            for a in range(2):
-                crossing(g, tau, a).wait_send()
-        each(lambda a, g: sideways(tau, a, g, 0).wait_send())
-        each(lambda a, g: sideways(tau, a, g, 1).wait_send())
-        each(lambda a, g: onward(tau, a, g).wait_send())
+        part_of = acts.at[0, pl.ds(0, 3)]
+        pltpu.make_async_copy(part_of, part_of, x_send.at[tau]).wait()
 
     @pl.loop(0, ALL)
     def _(p):
-        gather.finish(p)
+        @pl.when((p < PIECES) | (p >= PIECES + 2))
+        def _():
+            gather.finish(p)
+
+        @pl.when((p >= PIECES) & (p < PIECES + 2))
+        def _():
+            for a, buf in enumerate((all_normed, all_errors)):
+                there = buf.at[p]
+                pltpu.make_async_copy(there, there, send.at[p, a]).wait()
 
     @pl.loop(0, PIECES)
     def _(q):
@@ -651,13 +694,13 @@
         def _():
             m0(q).wait_send()
 
-        for m in (m1, m2, m3, m4, m5):
-            m(q).wait_send()
+        part_of = all_normed.at[0, pl.ds(0, 7 * HALF), :]
+        pltpu.make_async_copy(part_of, part_of, rs_send.at[q, 1]).wait()
 
     collect(2)
     for level in range(3):
-        for k in range(3):
-            spread(level, k).wait_send()
+        there = gains.at[level, pl.ds(0, 3)]
+        pltpu.make_async_copy(there, there, g_send.at[level]).wait()
     for tau in range(2):
         swap(tau).wait()
     for copy in emit(1):
@@ -681,7 +724,7 @@
         kernel,
         name="block",
         out_shape=(
-            shape((TOK, W * PIECES)), shape((8, W), F32),
+            shape((TOK, W * PIECES)), shape((1, W * PIECES), F32),
             shape((2 * W, W)), shape((W, 2 * W)),
         ),
         in_specs=[VM, VM, VM, ANY, ANY],
@@ -710,9 +753,8 @@
             bf16((6, HALF, WIDE)),
             f32((3, 4, 8, W)),
             *gather_scratch(ALL),
-            DMA((6, 2)), DMA((6, 2)), DMA((2, 2, 2, 2)), DMA((2, 2, 2, 2)),
-            DMA((2, 2, 2)), DMA((2, 2, 2)), DMA((2, 3)), DMA((2,)),
-            DMA((PIECES, 6)), DMA((PIECES, 6)), DMA((3, 3)), DMA((3, 3)),
+            DMA, DMA((6, 2)), DMA((2,)), DMA((2, 3)), DMA((2, 3)), DMA((2,)),
+            DMA((PIECES, 2)), DMA((PIECES, 4)), DMA((3,)), DMA((3,)),
             DMA((2,)), DMA((2,)),
         ],
         compiler_params=pltpu.CompilerParams(
@@ -724,7 +766,7 @@
 def emit_kernel(
     passed, gain, in_grad, out_grad,
     passed_out, gain_out, in_out, out_out,
-    a, b, load, save,
+    a, b, held_passed, held_gain, load, save,
 ):
     pairs = []
     for k in range(4):
@@ -732,21 +774,19 @@
         pairs.append((in_grad.at[rows, :], a.at[rows, :], in_out.at[rows, :]))
         rows = pl.ds(k * 192, 192)
         pairs.append((out_grad.at[rows, :], b.at[rows, :], out_out.at[rows, :]))
-    pairs.append((passed, passed_out, None))
+    pairs.append((passed, held_passed, passed_out))
+    pairs.append((gain, held_gain, gain_out))
     loads = [
         pltpu.make_async_copy(source, held, load.at[k])
         for k, (source, held, _) in enumerate(pairs)
     ]
     for copy in loads:
         copy.start()
-    for q in range(PIECES):
-        gain_out[:, pl.ds(q * W, W)] = gain[pl.ds(q, 1), :]
     saves = []
     for k, (_, held, out) in enumerate(pairs):
         loads[k].wait()
-        if out is not None:
-            saves.append(pltpu.make_async_copy(held, out, save.at[k]))
-            saves[-1].start()
+        saves.append(pltpu.make_async_copy(held, out, save.at[k]))
+        saves[-1].start()
     for copy in saves:
         copy.wait()
 
@@ -759,11 +799,12 @@
             shape((TOK, W * PIECES)), shape((1, W * PIECES), F32),
             shape((2 * W, W)), shape((W, 2 * W)),
         ),
-        in_specs=[ANY, VM, ANY, ANY],
-        out_specs=(VM, VM, ANY, ANY),
+        in_specs=[ANY, ANY, ANY, ANY],
+        out_specs=(ANY, ANY, ANY, ANY),
         scratch_shapes=[
             pltpu.VMEM((WIDE, W), BF16), pltpu.VMEM((W, WIDE), BF16),
-            DMA((9,)), DMA((9,)),
+            pltpu.VMEM((TOK, W * PIECES), BF16), pltpu.VMEM((1, W * PIECES), F32),
+            DMA((10,)), DMA((10,)),
         ],
     )(*results)
 

time: 141 us -> 133 us (0.943)
  Pallas kernels: 140 us -> 132 us
    pallas_call x1, Pallas kernels: 135 us -> 128 us  [block_call(): pl.pallas_call(kernel, name='block', out_shape=(shape((TOK, W * PIECES)),...]
where the time goes in v4:
time: 133 us
  Pallas kernels  132 us (99%)
    pallas_call x1, Pallas kernels, block_call(): pl.pallas_call(kernel, name='block', out_shape=(shape((TOK, W * PIECES)),...  128 us
    pallas_call x1, Pallas kernels, emit_call(): pl.pallas_call(emit_kernel, name='emit', out_shape=(shape((TOK, W * PIECE...  4.48 us

profile of v4, /device:TPU:0, one launch (start us, length us, event | category | flops | bytes accessed | tf_op | source)
XLA Modules:
  0.0 132.9 jit_solution(9943718867065902122)
XLA Ops:
  0.6 127.8 %block.1 = (bf16[32,6144]{1,0:T(8,128)(2,1)}, f32[1,6144]{1,0:T(1,128)}, bf16[1536,768]{1,0:T(8,128)(2,1)}, bf16[768,1536]{1,0:T(8,128)(2,1)}) custom-call(bf16[32,6144]{1,0:T(8,128)(2,1)} %bitcast.9, bf16[32,6144]{1,0:T(8,128)(2,1)} %bitcast.10, f32[1,6144]{1,0:T(1,128)} %gain.1, bf16[6144,768]{1,0:T(8,128)(2,1)} %bitcast.7, bf16[768,6144]{1,0:T(8,128)(2,1)} %bitcast.8), custom_call_target="tpu_custom_call" | custom-call | tf_op jit(solution)/shard_map/block/pallas_call | solution.py:723
  128.5 4.5 %emit.1 = (bf16[32,6144]{1,0:T(8,128)(2,1)}, f32[1,6144]{1,0:T(1,128)}, bf16[1536,768]{1,0:T(8,128)(2,1)}, bf16[768,1536]{1,0:T(8,128)(2,1)}) custom-call(bf16[32,6144]{1,0:T(8,128)(2,1)} %get-tuple-element.12.passed, f32[1,6144]{1,0:T(1,128)} %get-tuple-element.13.gain, bf16[1536,768]{1,0:T(8,128)(2,1)} %get-tuple-element.14.in_grad, ...), custom_call_target="tpu_custom_call" | custom-call | tf_op jit(solution)/shard_map/emit/pallas_call | solution.py:795

commit v5 on v4

--- a/solution.py
+++ b/solution.py
@@ -67,23 +67,22 @@
         return pltpu.make_async_remote_copy(
             src_ref=there if source is None else source,
             dst_ref=there,
-            send_sem=self.send.at[p, a],
+            send_sem=self.send.at[p],
             recv_sem=sem,
             device_id=target,
             device_id_type=MESH,
         )
 
     def put(self, stage, p, a, rows, target, source=None, cols=FULL):
-        sem = self.recv.at[p, a, stage]
+        sem = self.recv.at[p, stage]
         self.copy(p, a, rows, sem, target, source, cols).start()
 
-    def got(self, stage, p, a):
-        rows = pl.ds(0, (3, 3, 1)[stage] * HALF)
-        sem = self.recv.at[p, a, stage]
-        self.copy(p, a, rows, sem, neighbour(dz=1)).wait_recv()
+    def got(self, stage, p):
+        rows = pl.ds(0, (6, 6, 2)[stage] * HALF)
+        self.copy(p, 0, rows, self.recv.at[p, stage], neighbour(dz=1)).wait_recv()
 
     def to_core(self, p, a, dh, dz, source=None):
-        sem = self.core_recv.at[p, a]
+        sem = self.core_recv.at[p]
         self.copy(p, a, self.block(dh, dz), sem, neighbour(dc=1), source).start()
 
     def stage0(self, p, sources):
@@ -97,8 +96,8 @@
 
     def stage1(self, p):
         up, down, across = neighbour(dz=1), neighbour(dz=-1), neighbour(dh=1)
+        self.got(0, p)
         for a in range(2):
-            self.got(0, p, a)
             if a == 0:
                 self.put(1, p, 0, self.block(1, 0), up)
                 self.put(1, p, 0, self.block(1, 0), down)
@@ -113,8 +112,8 @@
 
     def stage2(self, p):
         up, down, across = neighbour(dz=1), neighbour(dz=-1), neighbour(dh=1)
+        self.got(1, p)
         for a in range(2):
-            self.got(1, p, a)
             if a == 0:
                 self.put(2, p, 0, self.block(1, 1), down, None, LEFT)
                 self.put(2, p, 0, self.block(1, -1), up, None, RIGHT)
@@ -125,27 +124,24 @@
             self.to_core(p, a, 0, 2)
 
     def stage3(self, p):
+        self.got(2, p)
         for a in range(2):
-            self.got(2, p, a)
             self.to_core(p, a, 1, 2)
 
     def stage4(self, p):
-        for a in range(2):
-            rows = pl.ds(0, 8 * HALF)
-            sem = self.core_recv.at[p, a]
-            self.copy(p, a, rows, sem, neighbour(dc=1)).wait_recv()
+        rows = pl.ds(0, 16 * HALF)
+        self.copy(p, 0, rows, self.core_recv.at[p], neighbour(dc=1)).wait_recv()
 
     def finish(self, p):
-        for a in range(2):
-            part = self.bufs[a].at[p, pl.ds(0, 15 * HALF), :]
-            pltpu.make_async_copy(part, part, self.send.at[p, a]).wait()
+        part = self.bufs[0].at[pl.ds(0, 2), pl.ds(0, 15 * HALF), :]
+        pltpu.make_async_copy(part, part, self.send.at[p]).wait()
 
 
 def gather_scratch(pieces):
     return [
-        pltpu.SemaphoreType.DMA((pieces, 2)),
-        pltpu.SemaphoreType.DMA((pieces, 2, 3)),
-        pltpu.SemaphoreType.DMA((pieces, 2)),
+        pltpu.SemaphoreType.DMA((pieces,)),
+        pltpu.SemaphoreType.DMA((pieces, 3)),
+        pltpu.SemaphoreType.DMA((pieces,)),
     ]
 
 
@@ -214,7 +210,7 @@
             src_ref=(normed, errors)[a].at[tokens(tau), cols],
             dst_ref=(slice_normed, slice_errors)[a].at[tau * 3 + g],
             send_sem=c_send,
-            recv_sem=c_recv.at[tau * 3 + g, a],
+            recv_sem=c_recv.at[tau * 3 + g],
             device_id=neighbour(dx=dx),
             device_id_type=MESH,
         )
@@ -229,46 +225,39 @@
 
     def stage0_slice(p):
         u = p - PIECES
-        for a, buf in enumerate((slice_normed, slice_errors)):
-            pltpu.make_async_remote_copy(
-                src_ref=buf.at[u],
-                dst_ref=buf.at[u],
-                send_sem=c_send,
-                recv_sem=c_recv.at[u, a],
-                device_id=right,
-                device_id_type=MESH,
-            ).wait_recv()
+        there = slice_normed.at[pl.ds(0, 2)]
+        pltpu.make_async_copy(there, there, c_recv.at[u]).wait()
         gather.stage0(p, (slice_normed.at[u], slice_errors.at[u]))
         own = gather.block(0, 0)
         all_normed[p, own, :] = slice_normed[u]
         all_errors[p, own, :] = slice_errors[u]
 
     def hand(p, g, act):
-        for a, buf in enumerate((all_normed, all_errors)):
+        for buf in (all_normed, all_errors):
             for i in range(8):
                 rows = pl.ds(pl.multiple_of((i * 2 + c) * HALF, HALF), HALF)
                 act(
                     pltpu.make_async_remote_copy(
                         src_ref=buf.at[p, rows, :],
                         dst_ref=buf.at[PIECES + g, rows, :],
-                        send_sem=send.at[PIECES + g, a],
-                        recv_sem=recv.at[PIECES + g, a, 0],
+                        send_sem=send.at[PIECES + g],
+                        recv_sem=recv.at[PIECES + g, 0],
                         device_id=(left, right)[g],
                         device_id_type=MESH,
                     )
                 )
 
     def handed(g):
-        for a, buf in enumerate((all_normed, all_errors)):
-            there = buf.at[PIECES + g, pl.ds(0, 8 * HALF), :]
-            pltpu.make_async_copy(there, there, recv.at[PIECES + g, a, 0]).wait()
+        there = all_normed.at[PIECES + g]
+        pltpu.make_async_copy(there, there, recv.at[PIECES + g, 0]).wait()
+        for buf in (all_normed, all_errors):
             for i in range(8):
                 rows = pl.ds(pl.multiple_of((i * 2 + c) * HALF, HALF), HALF)
                 pltpu.make_async_remote_copy(
                     src_ref=buf.at[PIECES + g, rows, :],
                     dst_ref=buf.at[PIECES + g, rows, :],
-                    send_sem=send.at[PIECES + g, a],
-                    recv_sem=core_recv.at[PIECES + g, a],
+                    send_sem=send.at[PIECES + g],
+                    recv_sem=core_recv.at[PIECES + g],
                     device_id=other,
                     device_id_type=MESH,
                 ).start()
@@ -593,21 +582,23 @@
         def _():
             handed(0)
 
-        @pl.when((t == 12) | (t == 15))
-        def _():
-            tau = (t - 12) // 3
+        @pl.when((t == 11) | (t == 15))
+        def _():
+            tau = (t - 11) // 4
             arrived(tau, 0)
             each(lambda a, g: onward(tau, a, g).start())
 
-        @pl.when((t == 14) | (t == 18))
-        def _():
-            tau = (t - 14) // 4
-            arrived(tau, 1)
+        @pl.when(t == 14)
+        def _():
+            arrived(0, 1)
 
         @pl.when(t == 16)
         def _():
+            correct(0)
+
+        @pl.when(t == 17)
+        def _():
             arrived(0, 2)
-            correct(0)
 
         @pl.when((t == 12) | (t == 13))
         def _():
@@ -632,7 +623,7 @@
             start_gain()
             correct(1)
 
-        @pl.when(t >= 15)
+        @pl.when((t >= 15) & (t < 18))
         def _():
             u = t - 15
             gather.stage4(PIECES + u)
@@ -641,7 +632,24 @@
             def _(half):
                 add_products(PIECES + u, u % 3, u // 3, half)
 
-    collect(0)
+    arrived(1, 1)
+
+    @pl.loop(3, 5)
+    def _(u):
+        gather.stage4(PIECES + u)
+
+        @pl.loop(0, 2)
+        def _(half):
+            add_products(PIECES + u, u - 3, 1, half)
+
+        @pl.when(u == 3)
+        def _():
+            collect(0)
+
+        @pl.when(u == 4)
+        def _():
+            collect(1)
+
     arrived(1, 2)
     gather.stage4(13)
 
@@ -666,10 +674,6 @@
         for copy in emit(half):
             copy.start()
 
-        @pl.when(half == 0)
-        def _():
-            collect(1)
-
     part_of = all_normed.at[0, pl.ds(0, 8 * HALF), :]
     pltpu.make_async_copy(part_of, part_of, c_send).wait()
     for tau in range(2):
@@ -684,9 +688,8 @@
 
         @pl.when((p >= PIECES) & (p < PIECES + 2))
         def _():
-            for a, buf in enumerate((all_normed, all_errors)):
-                there = buf.at[p]
-                pltpu.make_async_copy(there, there, send.at[p, a]).wait()
+            there = all_normed.at[pl.ds(0, 2)]
+            pltpu.make_async_copy(there, there, send.at[p]).wait()
 
     @pl.loop(0, PIECES)
     def _(q):
@@ -753,7 +756,7 @@
             bf16((6, HALF, WIDE)),
             f32((3, 4, 8, W)),
             *gather_scratch(ALL),
-            DMA, DMA((6, 2)), DMA((2,)), DMA((2, 3)), DMA((2, 3)), DMA((2,)),
+            DMA, DMA((6,)), DMA((2,)), DMA((2, 3)), DMA((2, 3)), DMA((2,)),
             DMA((PIECES, 2)), DMA((PIECES, 4)), DMA((3,)), DMA((3,)),
             DMA((2,)), DMA((2,)),
         ],

time: 133 us -> 131 us (0.985)
  Pallas kernels: 132 us -> 130 us
    pallas_call x1, Pallas kernels: 128 us -> 125 us  [block_call(): pl.pallas_call(kernel, name='block', out_shape=(shape((TOK, W * PIECES)),...]
where the time goes in v5:
time: 131 us
  Pallas kernels  130 us (99%)
    pallas_call x1, Pallas kernels, block_call(): pl.pallas_call(kernel, name='block', out_shape=(shape((TOK, W * PIECES)),...  125 us
    pallas_call x1, Pallas kernels, emit_call(): pl.pallas_call(emit_kernel, name='emit', out_shape=(shape((TOK, W * PIECE...  4.48 us

profile of v5, /device:TPU:0, one launch (start us, length us, event | category | flops | bytes accessed | tf_op | source)
XLA Modules:
  0.0 130.5 jit_solution(18153182554083670845)
XLA Ops:
  0.6 125.4 %block.1 = (bf16[32,6144]{1,0:T(8,128)(2,1)}, f32[1,6144]{1,0:T(1,128)}, bf16[1536,768]{1,0:T(8,128)(2,1)}, bf16[768,1536]{1,0:T(8,128)(2,1)}) custom-call(bf16[32,6144]{1,0:T(8,128)(2,1)} %bitcast.9, bf16[32,6144]{1,0:T(8,128)(2,1)} %bitcast.10, f32[1,6144]{1,0:T(1,128)} %gain.1, bf16[6144,768]{1,0:T(8,128)(2,1)} %bitcast.7, bf16[768,6144]{1,0:T(8,128)(2,1)} %bitcast.8), custom_call_target="tpu_custom_call" | custom-call | tf_op jit(solution)/shard_map/block/pallas_call | solution.py:726
  126.0 4.5 %emit.1 = (bf16[32,6144]{1,0:T(8,128)(2,1)}, f32[1,6144]{1,0:T(1,128)}, bf16[1536,768]{1,0:T(8,128)(2,1)}, bf16[768,1536]{1,0:T(8,128)(2,1)}) custom-call(bf16[32,6144]{1,0:T(8,128)(2,1)} %get-tuple-element.12.passed, f32[1,6144]{1,0:T(1,128)} %get-tuple-element.13.gain, bf16[1536,768]{1,0:T(8,128)(2,1)} %get-tuple-element.14.in_grad, ...), custom_call_target="tpu_custom_call" | custom-call | tf_op jit(solution)/shard_map/emit/pallas_call | solution.py:798

commit v6 on v5

--- a/solution.py
+++ b/solution.py
@@ -558,21 +558,21 @@
         def _():
             scatter4(t - 12)
 
-        @pl.when((t == 9) | ((t >= 13) & (t < 16)))
-        def _():
-            stage0_slice(t + 1 - 3 * (t // 13))
-
-        @pl.when((t == 10) | ((t >= 15) & (t < 18)))
-        def _():
-            gather.stage1(t - 4 * (t // 15))
-
-        @pl.when((t == 11) | ((t >= 16) & (t < 19)))
-        def _():
-            gather.stage2(t - 1 - 4 * (t // 16))
-
-        @pl.when((t == 12) | (t >= 17))
-        def _():
-            gather.stage3(t - 2 - 4 * (t // 17))
+        @pl.when((t == 9) | ((t >= 12) & (t < 15)))
+        def _():
+            stage0_slice(t + 1 - 2 * (t // 12))
+
+        @pl.when((t == 10) | ((t >= 14) & (t < 17)))
+        def _():
+            gather.stage1(t - 3 * (t // 14))
+
+        @pl.when((t == 11) | ((t >= 15) & (t < 18)))
+        def _():
+            gather.stage2(t - 1 - 3 * (t // 15))
+
+        @pl.when((t == 12) | ((t >= 16) & (t < 19)))
+        def _():
+            gather.stage3(t - 2 - 3 * (t // 16))
 
         @pl.when(t == 10)
         def _():

time: 131 us -> 128 us (0.977)
  Pallas kernels: 130 us -> 127 us
    pallas_call x1, Pallas kernels: 125 us -> 122 us  [block_call(): pl.pallas_call(kernel, name='block', out_shape=(shape((TOK, W * PIECES)),...]
where the time goes in v6:
time: 128 us
  Pallas kernels  127 us (99%)
    pallas_call x1, Pallas kernels, block_call(): pl.pallas_call(kernel, name='block', out_shape=(shape((TOK, W * PIECES)),...  122 us
    pallas_call x1, Pallas kernels, emit_call(): pl.pallas_call(emit_kernel, name='emit', out_shape=(shape((TOK, W * PIECE...  4.48 us

profile of v6, /device:TPU:0, one launch (start us, length us, event | category | flops | bytes accessed | tf_op | source)
XLA Modules:
  0.0 127.6 jit_solution(3400522101848543570)
XLA Ops:
  0.6 122.5 %block.1 = (bf16[32,6144]{1,0:T(8,128)(2,1)}, f32[1,6144]{1,0:T(1,128)}, bf16[1536,768]{1,0:T(8,128)(2,1)}, bf16[768,1536]{1,0:T(8,128)(2,1)}) custom-call(bf16[32,6144]{1,0:T(8,128)(2,1)} %bitcast.9, bf16[32,6144]{1,0:T(8,128)(2,1)} %bitcast.10, f32[1,6144]{1,0:T(1,128)} %gain.1, bf16[6144,768]{1,0:T(8,128)(2,1)} %bitcast.7, bf16[768,6144]{1,0:T(8,128)(2,1)} %bitcast.8), custom_call_target="tpu_custom_call" | custom-call | tf_op jit(solution)/shard_map/block/pallas_call | solution.py:726
  123.1 4.5 %emit.1 = (bf16[32,6144]{1,0:T(8,128)(2,1)}, f32[1,6144]{1,0:T(1,128)}, bf16[1536,768]{1,0:T(8,128)(2,1)}, bf16[768,1536]{1,0:T(8,128)(2,1)}) custom-call(bf16[32,6144]{1,0:T(8,128)(2,1)} %get-tuple-element.12.passed, f32[1,6144]{1,0:T(1,128)} %get-tuple-element.13.gain, bf16[1536,768]{1,0:T(8,128)(2,1)} %get-tuple-element.14.in_grad, ...), custom_call_target="tpu_custom_call" | custom-call | tf_op jit(solution)/shard_map/emit/pallas_call | solution.py:798
